TPU v7x, 32 devices: a whole 2x2x4 slice. The times are simulated.
32 devices in a mesh: blk: 16 (over z, y, core), rep: 2 (over x).
Axes of the slice: x: 2, y: 2, z: 4, core: 2. Of those that a mesh axis runs over, the one named last changes fastest.
Arguments:
- features: bfloat16 [16384, 256], P('blk'), may hold values from -6 to 6
- weight_self: bfloat16 [256, 256], replicated, may hold values from -0.375 to 0.375
- weight_neighbor: bfloat16 [256, 256], replicated, may hold values from -0.375 to 0.375
- bias_vector: float32 [256], replicated, may hold values from -3 to 3
- tile_row: int32 [16, 16, 64], P('blk', 'rep'), may hold values from 0 to 7
- tile_column: int32 [16, 16, 64], P('blk', 'rep'), may hold values from 0 to 7
- tile_value: int32 [16, 16, 64], P('blk', 'rep'), may hold values from 0 to 127
- tile_count: int32 [16, 16], P('blk', 'rep'), may hold values from 16 to 64
- tile_table: bfloat16 [4096, 128, 128], P(('blk', 'rep')), may hold values from -0.0625 to 0.0625
- cotangent: bfloat16 [16384, 256], P('blk'), may hold values from -6 to 6
Outputs:
- activations: bfloat16 [16384, 256], P('blk')
- grad_features: bfloat16 [16384, 256], P('blk')
- grad_weight_self: float32 [256, 256], replicated
- grad_weight_neighbor: float32 [256, 256], replicated
- grad_bias: float32 [256], replicated
All inputs are finite; a program needn't handle non-finite values.
Results may differ from a plain program's by a relative error of at most 0.025.
Values may be sent and summed in bfloat16 or wider, within the bound.
A program may use at most 64 MiB of HBM per device.

v0:
```python
import functools

import jax
import jax.numpy as jnp
from jax import lax
from jax.experimental import pallas as pl
from jax.experimental.pallas import tpu as pltpu
from jax.sharding import PartitionSpec as P

ROWS_ROWS = (((0,), (0,)), ((), ()))
COLS_COLS = (((1,), (1,)), ((), ()))


def build_kernel(rows, columns, values, counts, table, dense):
    step = pl.program_id(0)
    tile = table.shape[1]
    dense[...] = jnp.zeros_like(dense)

    def add_tile(slot, carry):
        row = pl.multiple_of(rows[step, slot] * tile, tile)
        column = pl.multiple_of(columns[step, slot] * tile, tile)
        place = (0, pl.ds(row, tile), pl.ds(column, tile))
        dense[place] = dense[place] + table[values[step, slot]]
        return carry

    lax.fori_loop(0, counts[step], add_tile, 0)


def build_dense(rows, columns, values, counts, table, row_total):
    step_count = rows.shape[0]
    return pl.pallas_call(
        build_kernel,
        grid_spec=pltpu.PrefetchScalarGridSpec(
            num_scalar_prefetch=4,
            grid=(step_count,),
            in_specs=[pl.BlockSpec(table.shape, lambda s, *_: (0, 0, 0))],
            out_specs=pl.BlockSpec((1, row_total, row_total), lambda s, *_: (s, 0, 0)),
        ),
        out_shape=jax.ShapeDtypeStruct((step_count, row_total, row_total), jnp.bfloat16),
        cost_estimate=pl.CostEstimate(
            flops=0, bytes_accessed=20 * 2**20, transcendentals=0
        ),
        name="build",
    )(rows, columns, values, counts, table)


def ring_place(cycle, replicas):
    group = lax.axis_index("blk")
    replica = lax.axis_index("rep")
    reverse = (2 * replica) // replicas if replicas > 1 else 0 * replica
    ahead = lax.rem(group + 1 - 2 * reverse + cycle, cycle)
    behind = lax.rem(group - 1 + 2 * reverse + cycle, cycle)
    return group, replica, reverse, ahead, behind


def greet(devices):
    barrier = pltpu.get_barrier_semaphore()
    for device in devices:
        pl.semaphore_signal(
            barrier, inc=1, device_id={"blk": device},
            device_id_type=pl.DeviceIdType.MESH,
        )
    pl.semaphore_wait(barrier, len(devices))


def forward_kernel(
    cycle, replicas, pieces, features, dense, out,
    slots, blocks, total, block_sem, first_sem, send_sem, recv_sem,
):
    steps, rows = blocks.shape[0], blocks.shape[1]
    _, _, reverse, ahead, behind = ring_place(cycle, replicas)
    size = rows // pieces
    first = pltpu.make_async_copy(features, slots.at[0], first_sem)
    first.start()

    def load(step):
        return pltpu.make_async_copy(
            dense.at[step], blocks.at[step], block_sem.at[step]
        )

    def in_order(hop):
        return hop * (1 - reverse) + (steps - hop) * reverse

    @pl.loop(0, steps)
    def _(hop):
        load(in_order(hop + reverse)).start()

    greet((ahead, behind))
    first.wait()

    def hop_copy(hop, piece):
        span = pl.ds(piece * size, size)
        return pltpu.make_async_remote_copy(
            src_ref=slots.at[hop, span],
            dst_ref=slots.at[hop + 1, span],
            send_sem=send_sem.at[hop, piece],
            recv_sem=recv_sem.at[hop, piece],
            device_id={"blk": ahead},
            device_id_type=pl.DeviceIdType.MESH,
        )

    total[...] = jnp.zeros_like(total)
    hops = steps - 1 + reverse

    @pl.loop(0, hops + 1)
    def _(hop):
        for piece in range(pieces):
            @pl.when(hop > 0)
            def _():
                hop_copy(hop - 1, piece).wait_recv()

            @pl.when(hop < hops)
            def _():
                hop_copy(hop, piece).start()

        step = in_order(hop)

        @pl.when(step < steps)
        def _():
            load(step).wait()
            total[...] += jnp.dot(
                blocks[step], slots[hop], preferred_element_type=jnp.float32
            )

    out[...] = total[...].astype(out.dtype)

    @pl.loop(0, hops)
    def _(hop):
        for piece in range(pieces):
            hop_copy(hop, piece).wait_send()


LANES = 4


def is_layered(cycle, replicas):
    return (
        cycle // replicas == 2 * LANES and cycle >= 3 * LANES
        and cycle % LANES == 0 and replicas == 2
    )


def forward(cycle, replicas, features, dense):
    step_count, row_total, _ = dense.shape
    width = features.shape[1]
    pieces = 4
    slots, sems = (step_count + 1, row_total, width), (step_count, pieces)
    return pl.pallas_call(
        functools.partial(forward_kernel, cycle, replicas, pieces),
        in_specs=[pl.BlockSpec(memory_space=pl.ANY)] * 2,
        out_specs=pl.BlockSpec(memory_space=pltpu.VMEM),
        out_shape=jax.ShapeDtypeStruct((row_total, width), jnp.bfloat16),
        scratch_shapes=[
            pltpu.VMEM(slots, jnp.bfloat16),
            pltpu.VMEM(dense.shape, jnp.bfloat16),
            pltpu.VMEM((row_total, width), jnp.float32),
            pltpu.SemaphoreType.DMA((step_count,)),
            pltpu.SemaphoreType.DMA,
            pltpu.SemaphoreType.DMA(sems),
            pltpu.SemaphoreType.DMA(sems),
        ],
        compiler_params=pltpu.CompilerParams(collective_id=0, has_side_effects=True),
        name="forward",
    )(features, dense)


def layer_kernel(
    features, mine, other, weight_self, weight_neighbor, bias, cotangent,
    activations, sent_t, self_t, grads,
):
    f32 = jnp.float32
    width = features.shape[1]
    aggregate = (mine[...].astype(f32) + other[...].astype(f32)).astype(jnp.bfloat16)
    pre = (
        jnp.dot(features[...], weight_self[...], preferred_element_type=f32)
        + jnp.dot(aggregate, weight_neighbor[...], preferred_element_type=f32)
        + bias[...]
    )
    sigmoid = jax.nn.sigmoid(pre)
    activations[...] = (pre * sigmoid).astype(activations.dtype)
    derivative = sigmoid * (1.0 + pre * (1.0 - sigmoid))
    grad_pre = (cotangent[...].astype(f32) * derivative).astype(jnp.bfloat16)
    sent_t[...] = lax.dot_general(
        weight_neighbor[...], grad_pre, COLS_COLS, preferred_element_type=f32
    ).astype(sent_t.dtype)
    self_t[...] = lax.dot_general(
        weight_self[...], grad_pre, COLS_COLS, preferred_element_type=f32
    )
    grad_self = lax.dot_general(
        features[...], grad_pre, ROWS_ROWS, preferred_element_type=f32
    ).astype(grads.dtype)
    grad_neighbor = lax.dot_general(
        aggregate, grad_pre, ROWS_ROWS, preferred_element_type=f32
    ).astype(grads.dtype)
    summed = jnp.sum(grad_pre.astype(f32), axis=0, keepdims=True)
    parts = grads.shape[0]
    depth = 2 * width // parts
    tail = grads.shape[1] - depth
    bias_rows = jnp.broadcast_to(summed, (tail, width)).astype(grads.dtype)
    for part in range(parts):
        source, place = (
            (grad_self, part) if 2 * part < parts else (grad_neighbor, part - parts // 2)
        )
        grads[part, 0:depth, :] = source[place * depth : (place + 1) * depth, :]
        grads[part, depth:, :] = bias_rows


def layer(parts, features, mine, other, weight_self, weight_neighbor, bias, cotangent):
    row_total, width = features.shape
    shape = jax.ShapeDtypeStruct
    return pl.pallas_call(
        layer_kernel,
        out_shape=(
            shape((row_total, width), jnp.bfloat16),
            shape((width, row_total), jnp.bfloat16),
            shape((width, row_total), jnp.float32),
            shape((parts, 2 * width // parts + 16, width), jnp.bfloat16),
        ),
        name="layer",
    )(features, mine, other, weight_self, weight_neighbor, bias, cotangent)


def backward_kernel(
    cycle, replicas, pieces, sent_t, dense, grads, out, part_out,
    landed, held, part_landed, part_held, blocks, term,
    block_sem, send_sem, recv_sem,
):
    steps = blocks.shape[0]
    width = sent_t.shape[0]
    size = width // pieces
    f32 = jnp.float32
    group, replica, reverse, behind, ahead = ring_place(cycle, replicas)

    def load(step):
        return pltpu.make_async_copy(
            dense.at[step], blocks.at[step], block_sem.at[step]
        )

    def in_order(hop):
        return (steps - 1 - hop) * (1 - reverse) + hop * reverse

    @pl.loop(0, steps)
    def _(hop):
        load(in_order(hop)).start()

    greet((ahead, behind))

    def hop_copy(hop, piece):
        if piece < pieces:
            span = pl.ds(piece * size, size)
            source, target = held.at[hop, span], landed.at[hop, span]
        else:
            source, target = part_held.at[hop], part_landed.at[hop]
        return pltpu.make_async_remote_copy(
            src_ref=source,
            dst_ref=target,
            send_sem=send_sem.at[hop, piece],
            recv_sem=recv_sem.at[hop, piece],
            device_id={"blk": ahead},
            device_id_type=pl.DeviceIdType.MESH,
        )

    hops = steps - 1 + reverse

    @pl.loop(0, steps)
    def _(hop):
        step = in_order(hop)
        target = lax.rem(group - steps * replica - step + 2 * cycle, cycle)
        load(step).wait()
        term[...] = jnp.dot(sent_t[...], blocks[step], preferred_element_type=f32)
        for piece in range(pieces + 1):
            span = pl.ds(piece * size, size)

            @pl.when(hop > 0)
            def _():
                hop_copy(hop - 1, piece).wait_recv()
                if piece < pieces:
                    held[hop, span] = (
                        term[span] + landed[hop - 1, span].astype(f32)
                    ).astype(held.dtype)
                else:
                    part_held[hop] = (
                        grads[target].astype(f32) + part_landed[hop - 1].astype(f32)
                    ).astype(part_held.dtype)

            @pl.when(hop == 0)
            def _():
                if piece < pieces:
                    held[hop, span] = term[span].astype(held.dtype)
                else:
                    part_held[hop] = grads[target]

            @pl.when(hop < hops)
            def _():
                hop_copy(hop, piece).start()

    @pl.when(reverse == 0)
    def _():
        out[...] = held[steps - 1]
        part_out[...] = part_held[steps - 1]

    @pl.when(reverse == 1)
    def _():
        for piece in range(pieces + 1):
            hop_copy(steps - 1, piece).wait_recv()
        out[...] = landed[steps - 1]
        part_out[...] = part_landed[steps - 1]

    @pl.loop(0, hops)
    def _(hop):
        for piece in range(pieces + 1):
            hop_copy(hop, piece).wait_send()


def backward(cycle, replicas, sent_t, dense, grads):
    step_count, row_total, _ = dense.shape
    width = sent_t.shape[0]
    part = grads.shape[1:]
    pieces = 4
    bf16 = jnp.bfloat16
    return pl.pallas_call(
        functools.partial(backward_kernel, cycle, replicas, pieces),
        in_specs=[
            pl.BlockSpec(memory_space=pltpu.VMEM),
            pl.BlockSpec(memory_space=pl.ANY),
            pl.BlockSpec(memory_space=pltpu.VMEM),
        ],
        out_specs=[pl.BlockSpec(memory_space=pltpu.VMEM)] * 2,
        out_shape=(
            jax.ShapeDtypeStruct((width, row_total), bf16),
            jax.ShapeDtypeStruct(part, bf16),
        ),
        scratch_shapes=[
            pltpu.VMEM((step_count, width, row_total), bf16),
            pltpu.VMEM((step_count, width, row_total), bf16),
            pltpu.VMEM((step_count, *part), bf16),
            pltpu.VMEM((step_count, *part), bf16),
            pltpu.VMEM(dense.shape, bf16),
            pltpu.VMEM((width, row_total), jnp.float32),
            pltpu.SemaphoreType.DMA((step_count,)),
            pltpu.SemaphoreType.DMA((step_count, pieces + 1)),
            pltpu.SemaphoreType.DMA((step_count, pieces + 1)),
        ],
        compiler_params=pltpu.CompilerParams(collective_id=1, has_side_effects=True),
        name="backward",
    )(sent_t, dense, grads)


def finish_kernel(
    cycle, replicas, pushed, part, self_t, weights, bias_out, grad_t,
    gathered, landed, part_landed, pair_send, pair_recv, send_sem, recv_sem,
):
    f32 = jnp.float32
    depth = gathered.shape[1]
    group = lax.axis_index("blk")
    partner = {"rep": lax.rem(lax.axis_index("rep") + replicas // 2, replicas)}
    mesh_id = pl.DeviceIdType.MESH
    barrier = pltpu.get_barrier_semaphore()
    pl.semaphore_signal(barrier, inc=1, device_id=partner, device_id_type=mesh_id)
    for away in range(1, cycle):
        pl.semaphore_signal(
            barrier, inc=1, device_id={"blk": lax.rem(group + away, cycle)},
            device_id_type=mesh_id,
        )
    pl.semaphore_wait(barrier, cycle)

    def swap(source, target, index):
        return pltpu.make_async_remote_copy(
            src_ref=source, dst_ref=target,
            send_sem=pair_send.at[index], recv_sem=pair_recv.at[index],
            device_id=partner, device_id_type=mesh_id,
        )

    part_swap = swap(part, part_landed, 0)
    part_swap.start()
    panel_swap = swap(pushed, landed, 1)
    panel_swap.start()
    part_swap.wait()
    summed = part[...].astype(f32) + part_landed[...].astype(f32)
    bias_out[...] = summed[depth:]
    gathered[group] = summed[:depth].astype(gathered.dtype)

    def put(away):
        return pltpu.make_async_remote_copy(
            src_ref=gathered.at[group],
            dst_ref=gathered.at[group],
            send_sem=send_sem.at[away],
            recv_sem=recv_sem.at[away],
            device_id={"blk": lax.rem(group + away, cycle)},
            device_id_type=mesh_id,
        )

    @pl.loop(1, cycle)
    def _(away):
        put(away).start()

    @pl.loop(1, cycle)
    def _(away):
        put(away).wait()

    weights[...] = gathered[...].astype(f32)
    panel_swap.wait()
    grad_t[...] = (
        self_t[...] + (pushed[...].astype(f32) + landed[...].astype(f32))
    ).astype(grad_t.dtype)


def finish(cycle, replicas, pushed, part, self_t):
    width = pushed.shape[0]
    depth = 2 * width // cycle
    tail = part.shape[0] - depth
    shape = jax.ShapeDtypeStruct
    return pl.pallas_call(
        functools.partial(finish_kernel, cycle, replicas),
        in_specs=[pl.BlockSpec(memory_space=pltpu.VMEM)] * 3,
        out_specs=[pl.BlockSpec(memory_space=pltpu.VMEM)] * 3,
        out_shape=(
            shape((cycle, depth, width), jnp.float32),
            shape((tail, width), jnp.float32),
            shape(pushed.shape, jnp.bfloat16),
        ),
        scratch_shapes=[
            pltpu.VMEM((cycle, depth, width), jnp.bfloat16),
            pltpu.VMEM(pushed.shape, jnp.bfloat16),
            pltpu.VMEM(part.shape, jnp.bfloat16),
            pltpu.SemaphoreType.DMA((2,)),
            pltpu.SemaphoreType.DMA((2,)),
            pltpu.SemaphoreType.DMA((cycle,)),
            pltpu.SemaphoreType.DMA((cycle,)),
        ],
        compiler_params=pltpu.CompilerParams(collective_id=2, has_side_effects=True),
        name="finish",
    )(pushed, part, self_t)


class Spot:
    def __init__(self, cycle, steps):
        self.steps, self.layers = steps, cycle // LANES
        self.group, self.replica = lax.axis_index("blk"), lax.axis_index("rep")
        self.sign = 1 - 2 * self.replica
        self.layer, self.lane = self.group // LANES, lax.rem(self.group, LANES)
        self.pair, self.core = self.lane // 2, lax.rem(self.lane, 2)
        self.lane_across = (1 - self.pair) * 2 + self.core
        self.lane_beside = self.pair * 2 + 1 - self.core
        self.across = self.layer * LANES + self.lane_across
        self.beside = self.layer * LANES + self.lane_beside

    def layer_at(self, distance):
        return lax.rem(self.layer + distance + 2 * self.layers, self.layers)

    def at_layer(self, distance):
        return self.layer_at(distance) * LANES + self.lane

    def step(self, lane, other_lane, distance):
        return (
            self.replica * self.steps + lane - other_lane
            + self.sign * LANES * distance
        )

    def meets(self, lane, other_lane, distance):
        step = self.step(lane, other_lane, distance)
        return jnp.logical_and(step >= 0, step < self.steps)

    def chip_meets(self, pair, other_lane, distance):
        return jnp.logical_or(
            self.meets(2 * pair, other_lane, distance),
            self.meets(2 * pair + 1, other_lane, distance),
        )

    def layer_meets(self, other_lane, distance):
        return jnp.logical_or(
            self.chip_meets(0, other_lane, distance),
            self.chip_meets(1, other_lane, distance),
        )

    def greet(self):
        barrier = pltpu.get_barrier_semaphore()
        signal = functools.partial(
            pl.semaphore_signal, barrier, inc=1, device_id_type=pl.DeviceIdType.MESH
        )
        signal(device_id={"blk": self.across})
        signal(device_id={"blk": self.beside})
        signal(device_id={"rep": 1 - self.replica})
        for away in range(1, self.layers):
            signal(device_id={"blk": self.at_layer(away)})
        pl.semaphore_wait(barrier, 2 + self.layers)


def remote(source, target, sems, index, device):
    send, recv = sems
    return pltpu.make_async_remote_copy(
        src_ref=source, dst_ref=target,
        send_sem=send.at[index], recv_sem=recv.at[index],
        device_id=device, device_id_type=pl.DeviceIdType.MESH,
    )


def layered_backward_kernel(
    cycle, pieces, sent_t, self_t, dense, grads,
    grad_out, weight_self_out, weight_neighbor_out, bias_out,
    blocks, acc, core_out, core_in, pair_out, pair_in, layer_out, layer_in,
    rep_out, rep_in, far_out, far_in, part_acc, core_part, pair_part_out, pair_part,
    layer_part_out, layer_part, rep_part_out, rep_part, gathered, block_sem,
    *sems,
):
    f32 = jnp.float32
    bf16 = jnp.bfloat16
    steps, rows = blocks.shape[0], blocks.shape[1]
    size = rows // pieces
    at = Spot(cycle, steps)
    layers = at.layers
    depth = gathered.shape[2]
    (core_sems, pair_sems, layer_sems, rep_sems, core_part_sems, pair_part_sems,
     layer_part_sems, rep_part_sems, spread_sems, widen_sems, far_sems) = [
        (sems[2 * k], sems[2 * k + 1]) for k in range(11)
    ]
    by_layer = pieces // 2
    partner = {"rep": 1 - at.replica}
    onward = {"blk": at.at_layer(-at.sign)}

    def load(step):
        return pltpu.make_async_copy(
            dense.at[step], blocks.at[step], block_sem.at[step]
        )

    @pl.loop(0, steps)
    def _(hop):
        load((steps - 1 - hop) * (1 - at.replica) + hop * at.replica).start()

    at.greet()

    def own_lane(side):
        return 2 * side + at.core

    def other_lane(side):
        return 2 * side + 1 - at.core

    def span(n):
        return pl.ds(pl.multiple_of(n * size, size), size)

    def core_copy(i, side):
        return remote(core_out.at[i, side], core_in.at[i, side], core_sems, (i, side),
                      {"blk": at.beside})

    def pair_copy(i):
        return remote(pair_out.at[i], pair_in.at[i], pair_sems, i, {"blk": at.across})

    def layer_copy(i):
        return remote(layer_out.at[i], layer_in.at[i], layer_sems, i, onward)

    def far_copy(n):
        return remote(far_out.at[n], far_in.at[n], far_sems, n, onward)

    def rep_copy(n):
        return remote(rep_out.at[n], rep_in.at[n], rep_sems, n, partner)

    def part_of(d, lane):
        return at.layer_at(-at.sign * d) * LANES + lane

    def core_part_copy(d, side):
        return remote(grads.at[part_of(d, other_lane(side))], core_part.at[d, side],
                      core_part_sems, (d, side), {"blk": at.beside})

    def pair_part_copy(d):
        return remote(pair_part_out.at[d], pair_part.at[d], pair_part_sems, d,
                      {"blk": at.across})

    def layer_part_copy(d):
        return remote(layer_part_out.at[d - 1], layer_part.at[d - 1], layer_part_sems,
                      d - 1, onward)

    def rep_part_copy():
        return remote(rep_part_out, rep_part, rep_part_sems, 0, partner)

    def spread(away):
        here = gathered.at[at.lane, at.layer]
        return remote(here, here, spread_sems, away, {"blk": at.at_layer(away)})

    def widen(k):
        lane = at.lane_across if k == 2 else at.lane
        device = at.across if k == 0 else at.beside
        return remote(gathered.at[lane], gathered.at[lane], widen_sems, k,
                      {"blk": device})

    def sends_core(d, side):
        return at.meets(at.lane, other_lane(side), d)

    def gets_core(d, side):
        return at.meets(at.lane_beside, own_lane(side), d)

    def early(d, n):
        return jnp.logical_and(d == 2, n < by_layer)

    def sends_far(n):
        return jnp.logical_and(n < by_layer, at.chip_meets(at.pair, at.lane_across, 2))

    def sends_pair(d, n=None):
        here = at.chip_meets(at.pair, at.lane_across, d)
        if n is None:
            return here
        return jnp.logical_and(here, jnp.logical_not(early(d, n)))

    def gets_pair(d, n=None):
        there = at.chip_meets(1 - at.pair, at.lane, d)
        if n is None:
            return there
        return jnp.logical_and(there, jnp.logical_not(early(d, n)))

    def sends_layer(d, n=None):
        far = at.layer_meets(at.lane, 2)
        if n is not None:
            far = jnp.logical_or(
                at.chip_meets(at.pair, at.lane, 2),
                jnp.logical_and(far, n >= by_layer),
            )
        return jnp.logical_and(d > 0, jnp.logical_or(d == 1, far))

    def gets_layer(d, n):
        return jnp.logical_and(d < 2, sends_layer(d + 1, n))

    def product(i, d, n, lane, store):
        step = at.step(at.lane, lane, d)

        @pl.when(n == 0)
        def _():
            load(step).wait()

        wide = pl.ds(pl.multiple_of(n * size, 2 * size), 2 * size)
        value = jnp.dot(
            sent_t[...], blocks[step, :, wide], preferred_element_type=f32
        )
        store(i, value[:, :size])
        store(i + 1, value[:, size:])

    def begin(i):
        d, n = 2 - i // pieces, lax.rem(i, pieces)
        for side in range(2):
            @pl.when(sends_core(d, side))
            def _():
                def store(i, value):
                    core_out[i, side] = value.astype(bf16)

                product(i, d, n, other_lane(side), store)
                core_copy(i, side).start()
                core_copy(i + 1, side).start()

        for side in range(2):
            own = at.meets(at.lane, own_lane(side), d)

            @pl.when(own)
            def _():
                def store(i, value):
                    acc[i, side] = value

                product(i, d, n, own_lane(side), store)

            @pl.when(jnp.logical_not(own))
            def _():
                for k in range(2):
                    acc[i + k, side] = jnp.zeros(acc.shape[2:], f32)

    def over_pair(i):
        d, n = 2 - i // pieces, lax.rem(i, pieces)
        for side in range(2):
            @pl.when(gets_core(d, side))
            def _():
                core_copy(i, side).wait_recv()
                acc[i, side] += core_in[i, side].astype(f32)

        @pl.when(jnp.logical_and(d == 2, sends_far(n)))
        def _():
            far_out[n] = acc[i, 1 - at.pair].astype(bf16)
            far_copy(n).start()

        @pl.when(jnp.logical_and(d == 1, sends_far(n)))
        def _():
            far_copy(n).wait_recv()
            acc[i, 1 - at.pair] += far_in[n].astype(f32)

        @pl.when(sends_pair(d, n))
        def _():
            pair_out[i] = acc[i, 1 - at.pair].astype(bf16)
            pair_copy(i).start()

    def over_layers(i):
        d, n = 2 - i // pieces, lax.rem(i, pieces)

        @pl.when(gets_pair(d, n))
        def _():
            pair_copy(i).wait_recv()
            acc[i, at.pair] += pair_in[i].astype(f32)

        @pl.when(gets_layer(d, n))
        def _():
            layer_copy(i - pieces).wait_recv()
            acc[i, at.pair] += layer_in[i - pieces].astype(f32)

        @pl.when(sends_layer(d, n))
        def _():
            layer_out[i] = acc[i, at.pair].astype(bf16)
            layer_copy(i).start()

        @pl.when(d == 0)
        def _():
            rep_out[n] = acc[i, at.pair].astype(bf16)
            rep_copy(n).start()

            @pl.when(n > 0)
            def _():
                close(n - 1)

    def parts_to_core():
        for d in range(3):
            for side in range(2):
                pl.when(sends_core(d, side))(
                    lambda: core_part_copy(d, side).start()
                )

    def parts_to_pair():
        for d in range(3):
            for side in range(2):
                own = at.meets(at.lane, own_lane(side), d)
                part_acc[d, side] = grads[part_of(d, own_lane(side))].astype(
                    f32
                ) * own.astype(f32)

                @pl.when(gets_core(d, side))
                def _():
                    core_part_copy(d, side).wait_recv()
                    part_acc[d, side] += core_part[d, side].astype(f32)

            @pl.when(sends_pair(d))
            def _():
                pair_part_out[d] = part_acc[d, 1 - at.pair].astype(bf16)
                pair_part_copy(d).start()

    def part_onward(d):
        @pl.when(gets_pair(d))
        def _():
            pair_part_copy(d).wait_recv()
            part_acc[d, at.pair] += pair_part[d].astype(f32)

        if d < 2:
            @pl.when(sends_layer(d + 1))
            def _():
                layer_part_copy(d + 1).wait_recv()
                part_acc[d, at.pair] += layer_part[d].astype(f32)

        if d > 0:
            @pl.when(sends_layer(d))
            def _():
                layer_part_out[d - 1] = part_acc[d, at.pair].astype(bf16)
                layer_part_copy(d).start()
        else:
            rep_part_out[...] = part_acc[0, at.pair].astype(bf16)
            rep_part_copy().start()

    def part_spread():
        rep_part_copy().wait_recv()
        summed = rep_part_out[...].astype(f32) + rep_part[...].astype(f32)
        bias_out[...] = summed[depth : depth + 1]
        gathered[at.lane, at.layer] = summed[:depth].astype(bf16)
        for away in range(1, layers):
            spread(away).start()

    def part_over_pair():
        for away in range(1, layers):
            spread(away).wait_recv()
        widen(0).start()

    def part_over_core():
        widen(0).wait_recv()
        widen(1).start()
        widen(2).start()

    def close(n):
        rep_copy(n).wait_recv()
        total = (
            self_t[:, span(n)] + rep_out[n].astype(f32) + rep_in[n].astype(f32)
        )
        grad_out[span(n), :] = total.T.astype(grad_out.dtype)

    timetable = (
        (0, parts_to_core),
        (2, parts_to_pair),
        (pieces + 2, functools.partial(part_onward, 2)),
        (2 * pieces + 1, functools.partial(part_onward, 1)),
        (2 * pieces + 3, functools.partial(part_onward, 0)),
        (3 * pieces, part_spread),
        (3 * pieces + 2, part_over_pair),
        (3 * pieces + 3, part_over_core),
    )

    @pl.loop(0, 4 * pieces)
    def _(i):
        @pl.when(jnp.logical_and(i < 3 * pieces, lax.rem(i, 2) == 0))
        def _():
            begin(i)

        @pl.when(jnp.logical_and(i > 0, i <= 3 * pieces))
        def _():
            over_pair(i - 1)

        @pl.when(i >= pieces)
        def _():
            over_layers(i - pieces)

        for turn, act in timetable:
            pl.when(i == turn)(act)

    widen(1).wait_recv()
    widen(2).wait_recv()
    per_weight = cycle // 2
    for layer in range(layers):
        for lane in range(LANES):
            part = layer * LANES + lane
            out = weight_self_out if part < per_weight else weight_neighbor_out
            place = part % per_weight * depth
            out[place : place + depth, :] = gathered[lane, layer].astype(f32)
    close(pieces - 1)

    @pl.loop(0, 3 * pieces)
    def _(i):
        d, n = 2 - i // pieces, lax.rem(i, pieces)

        for side in range(2):
            pl.when(sends_core(d, side))(lambda: core_copy(i, side).wait_send())
        pl.when(sends_pair(d, n))(lambda: pair_copy(i).wait_send())
        pl.when(sends_layer(d, n))(lambda: layer_copy(i).wait_send())

        @pl.when(d == 0)
        def _():
            rep_copy(n).wait_send()
            pl.when(sends_far(n))(lambda: far_copy(n).wait_send())

    for d in range(3):
        for side in range(2):
            pl.when(sends_core(d, side))(lambda: core_part_copy(d, side).wait_send())
        pl.when(sends_pair(d))(lambda: pair_part_copy(d).wait_send())
        if d > 0:
            pl.when(sends_layer(d))(lambda: layer_part_copy(d).wait_send())
    rep_part_copy().wait_send()
    for away in range(1, layers):
        spread(away).wait_send()
    for k in range(3):
        widen(k).wait_send()


def layered_backward(cycle, sent_t, self_t, dense, grads):
    step_count, row_total, _ = dense.shape
    width = sent_t.shape[0]
    part = grads.shape[1:]
    depth = 2 * width // cycle
    pieces = 4
    panel = (width, row_total // pieces)
    bf16, f32 = jnp.bfloat16, jnp.float32
    layers = cycle // LANES
    turns = 3 * pieces
    sems = [
        (turns, 2), (turns,), (2 * pieces,), (pieces,), (3, 2), (3,), (2,), (1,),
        (layers,), (3,), (pieces // 2,),
    ]
    vmem = pl.BlockSpec(memory_space=pltpu.VMEM)
    return pl.pallas_call(
        functools.partial(layered_backward_kernel, cycle, pieces),
        in_specs=[vmem, vmem, pl.BlockSpec(memory_space=pl.ANY), vmem],
        out_specs=[vmem] * 4,
        out_shape=(
            jax.ShapeDtypeStruct((row_total, width), bf16),
            jax.ShapeDtypeStruct((width, width), f32),
            jax.ShapeDtypeStruct((width, width), f32),
            jax.ShapeDtypeStruct((1, width), f32),
        ),
        scratch_shapes=[
            pltpu.VMEM(dense.shape, bf16),
            pltpu.VMEM((turns, 2, *panel), f32),
            pltpu.VMEM((turns, 2, *panel), bf16),
            pltpu.VMEM((turns, 2, *panel), bf16),
            pltpu.VMEM((turns, *panel), bf16),
            pltpu.VMEM((turns, *panel), bf16),
            pltpu.VMEM((2 * pieces, *panel), bf16),
            pltpu.VMEM((2 * pieces, *panel), bf16),
            pltpu.VMEM((pieces, *panel), bf16),
            pltpu.VMEM((pieces, *panel), bf16),
            pltpu.VMEM((pieces // 2, *panel), bf16),
            pltpu.VMEM((pieces // 2, *panel), bf16),
            pltpu.VMEM((3, 2, *part), f32),
            pltpu.VMEM((3, 2, *part), bf16),
            pltpu.VMEM((3, *part), bf16),
            pltpu.VMEM((3, *part), bf16),
            pltpu.VMEM((2, *part), bf16),
            pltpu.VMEM((2, *part), bf16),
            pltpu.VMEM(part, bf16),
            pltpu.VMEM(part, bf16),
            pltpu.VMEM((LANES, layers, depth, width), bf16),
            pltpu.SemaphoreType.DMA((step_count,)),
        ] + [pltpu.SemaphoreType.DMA(shape) for shape in sems for _ in range(2)],
        compiler_params=pltpu.CompilerParams(
            collective_id=3, has_side_effects=True, vmem_limit_bytes=44 * 2**20
        ),
        name="layered_backward",
    )(sent_t, self_t, dense, grads)


def layered_front_kernel(
    cycle, pieces, features, behind, across, dense,
    weight_self, weight_neighbor, bias, cotangent,
    activations, sent_t, self_t, grads,
    slots, blocks, total, rep_out, rep_in, sums, first_sem, block_sem, *sems,
):
    f32, bf16 = jnp.float32, jnp.bfloat16
    steps, rows = blocks.shape[0], blocks.shape[1]
    halves, half = total.shape[0], total.shape[2]
    size = rows // pieces
    at = Spot(cycle, steps)
    lane = at.lane
    diagonal = (1 - at.pair) * 2 + 1 - at.core
    layer_sems, pair_sems, core_sems, relay_sems, rep_sems, far_sems = [
        (sems[2 * k], sems[2 * k + 1]) for k in range(6)
    ]
    by_pair = pieces // 4
    partner = {"rep": 1 - at.replica}
    onward = {"blk": at.at_layer(at.sign)}

    def first(h, k):
        source, place = (
            (features, (0, lane)), (behind, (1, lane)), (across, (0, at.lane_across))
        )[k]
        return pltpu.make_async_copy(
            source.at[:, h * half : (h + 1) * half], slots.at[(*place, h)],
            first_sem.at[h, k],
        )

    for h in range(halves):
        for k in range(3):
            first(h, k).start()

    def load(step):
        return pltpu.make_async_copy(
            dense.at[step], blocks.at[step], block_sem.at[step]
        )

    @pl.loop(0, steps)
    def _(hop):
        load((steps - 1 - hop) * at.replica + hop * (1 - at.replica)).start()

    at.greet()
    for h in range(halves):
        for k in range(3):
            first(h, k).wait()

    def span(piece):
        return pl.ds(pl.multiple_of(piece * size, size), size)

    def layer_copy(h, d, p):
        return remote(slots.at[d, lane, h, span(p)], slots.at[d + 1, lane, h, span(p)],
                      layer_sems, (h, d, p), onward)

    def spot_copy(which, h, d, p):
        whose = at.lane_across if which == "relay" else lane
        here = slots.at[d, whose, h, span(p)]
        pack = {"pair": pair_sems, "core": core_sems, "relay": relay_sems}[which]
        device = at.across if which == "pair" else at.beside
        return remote(here, here, pack, (h, d, p), {"blk": device})

    def rep_copy(h, p):
        return remote(rep_out.at[h, span(p)], rep_in.at[h, span(p)], rep_sems, (h, p),
                      partner)

    def far_copy(h, p):
        whose = at.lane_across
        return remote(slots.at[1, whose, h, span(p)], slots.at[2, whose, h, span(p)],
                      far_sems, (h, p), onward)

    def sends_layer(p):
        return jnp.logical_or(
            at.chip_meets(at.pair, lane, 2),
            jnp.logical_and(p < by_pair, at.layer_meets(lane, 2)),
        )

    def sends_far(p):
        return jnp.logical_and(p >= by_pair, gets["pair"](2))

    def over_pair(d, p, kind):
        holds = kind["pair"](d)
        return jnp.logical_and(p < by_pair, holds) if d == 2 else holds

    sends = {
        "pair": lambda d: at.chip_meets(1 - at.pair, lane, d),
        "core": lambda d: at.meets(at.lane_beside, lane, d),
        "relay": lambda d: at.meets(at.lane_beside, at.lane_across, d),
    }
    gets = {
        "pair": lambda d: at.chip_meets(at.pair, at.lane_across, d),
        "core": lambda d: at.meets(lane, at.lane_beside, d),
        "relay": lambda d: at.meets(lane, diagonal, d),
    }

    def give(h, d, p, kinds):
        if "layer" in kinds:
            pl.when(sends_layer(p))(lambda: layer_copy(h, d, p).start())
        if "pair" in kinds:
            pl.when(over_pair(d, p, sends))(
                lambda: spot_copy("pair", h, d, p).start()
            )
        if "core" in kinds:
            pl.when(sends["core"](d))(lambda: spot_copy("core", h, d, p).start())

    def give_all(h, d, kinds):
        @pl.loop(0, pieces)
        def _(p):
            give(h, d, p, kinds)

    def arrive(h):
        @pl.loop(0, pieces)
        def _(p):
            @pl.when(sends_layer(p))
            def _():
                layer_copy(h, 1, p).wait_recv()
                give(h, 2, p, ("pair", "core"))

    def relay(h, d, then=None):
        @pl.loop(0, pieces)
        def _(p):
            @pl.when(gets["pair"](d))
            def _():
                if d > 0:
                    pl.when(over_pair(d, p, gets))(
                        lambda: spot_copy("pair", h, d, p).wait_recv()
                    )
                if d == 1:
                    pl.when(sends_far(p))(lambda: far_copy(h, p).start())
                if d == 2:
                    pl.when(sends_far(p))(lambda: far_copy(h, p).wait_recv())
                pl.when(sends["relay"](d))(
                    lambda: spot_copy("relay", h, d, p).start()
                )

            if then is not None:
                then(p)

    def gathered(h, d):
        for which in ("core", "relay"):
            @pl.when(gets[which](d))
            def _():
                @pl.loop(0, pieces)
                def _(p):
                    spot_copy(which, h, d, p).wait_recv()

    def multiply(h, d, place):
        @pl.loop(0, LANES)
        def _(source):
            step = at.step(lane, source, d)

            @pl.when(at.meets(lane, source, d))
            def _():
                total[h, place, :] += jnp.dot(
                    blocks[step, place, :], slots[d, source, h],
                    preferred_element_type=f32,
                )

    def await_blocks(d):
        @pl.loop(0, LANES)
        def _(source):
            @pl.when(at.meets(lane, source, d))
            def _():
                load(at.step(lane, source, d)).wait()

    def whole(h, d):
        gathered(h, d)
        if h == 0:
            await_blocks(d)
        multiply(h, d, slice(None))

    def last(h):
        gathered(h, 2)
        if h == 0:
            await_blocks(2)

        @pl.loop(0, pieces)
        def _(p):
            multiply(h, 2, span(p))
            rep_out[h, span(p)] = total[h, span(p)].astype(bf16)
            rep_copy(h, p).start()

    give_all(0, 1, ("layer", "pair", "core"))
    for h in range(halves):
        give_all(h, 0, ("core",))
        relay(h, 0)
    total[...] = jnp.zeros_like(total)
    sums[...] = jnp.zeros_like(sums)
    whole(0, 0)
    relay(0, 1, lambda p: give(1, 1, p, ("pair", "core")))
    give_all(1, 1, ("layer",))
    arrive(0)
    whole(0, 1)
    relay(1, 1)
    relay(0, 2)
    last(0)
    arrive(1)
    whole(1, 0)
    whole(1, 1)
    relay(1, 2)
    last(1)

    def joined(ref, place):
        return jnp.concatenate([ref[h, place] for h in range(halves)], axis=1)

    width = halves * half

    @pl.loop(0, pieces)
    def _(p):
        place = span(p)
        for h in range(halves):
            rep_copy(h, p).wait_recv()
        mine, other = joined(rep_out, place), joined(rep_in, place)
        aggregate = (mine.astype(f32) + other.astype(f32)).astype(bf16)
        own_rows = jnp.concatenate(
            [slots[0, lane, h, place] for h in range(halves)], axis=1
        )
        pre = (
            jnp.dot(own_rows, weight_self[...], preferred_element_type=f32)
            + jnp.dot(aggregate, weight_neighbor[...], preferred_element_type=f32)
            + bias[...]
        )
        sigmoid = jax.nn.sigmoid(pre)
        activations[place, :] = (pre * sigmoid).astype(activations.dtype)
        derivative = sigmoid * (1.0 + pre * (1.0 - sigmoid))
        grad_pre = (cotangent[place, :].astype(f32) * derivative).astype(bf16)
        sent_t[:, place] = lax.dot_general(
            weight_neighbor[...], grad_pre, COLS_COLS, preferred_element_type=f32
        ).astype(sent_t.dtype)
        self_t[:, place] = lax.dot_general(
            weight_self[...], grad_pre, COLS_COLS, preferred_element_type=f32
        )
        sums[0:width] += lax.dot_general(
            own_rows, grad_pre, ROWS_ROWS, preferred_element_type=f32
        )
        sums[width : 2 * width] += lax.dot_general(
            aggregate, grad_pre, ROWS_ROWS, preferred_element_type=f32
        )
        sums[2 * width : 2 * width + 1] += jnp.sum(
            grad_pre.astype(f32), axis=0, keepdims=True
        )

    parts = grads.shape[0]
    depth = 2 * width // parts
    tail = grads.shape[1] - depth
    bias_rows = jnp.broadcast_to(
        sums[2 * width : 2 * width + 1], (tail, width)
    ).astype(grads.dtype)
    for part in range(parts):
        grads[part, 0:depth, :] = sums[part * depth : (part + 1) * depth].astype(
            grads.dtype
        )
        grads[part, depth:, :] = bias_rows

    @pl.loop(0, pieces)
    def _(p):
        for h in range(halves):
            for d in range(3):
                if d == 1:
                    pl.when(sends_layer(p))(lambda: layer_copy(h, d, p).wait_send())
                    pl.when(sends_far(p))(lambda: far_copy(h, p).wait_send())
                if d > 0:
                    pl.when(over_pair(d, p, sends))(
                        lambda: spot_copy("pair", h, d, p).wait_send()
                    )
                for which in ("core", "relay"):
                    pl.when(sends[which](d))(
                        lambda: spot_copy(which, h, d, p).wait_send()
                    )
            rep_copy(h, p).wait_send()


def ahead_of_build(cycle, features):
    layers, places = cycle // LANES, [(g, r) for g in range(cycle) for r in range(2)]
    behind, across = [], []
    for group, replica in places:
        sign = 1 - 2 * replica
        layer, lane = group // LANES, group % LANES
        target = (layer + sign) % layers * LANES + lane
        behind.append((group * 2 + replica, target * 2 + replica))
        if lane // 2 == replica:
            target = layer * LANES + (lane + 2) % LANES
            across.append((group * 2 + replica, target * 2 + replica))
    return [lax.ppermute(features, ("blk", "rep"), pairs) for pairs in (behind, across)]


def layered_front(
    cycle, features, behind, across, dense, weight_self, weight_neighbor, bias, cotangent
):
    step_count, row_total, _ = dense.shape
    width = features.shape[1]
    pieces, halves = 4, 2
    half = width // halves
    bf16, f32 = jnp.bfloat16, jnp.float32
    shape = jax.ShapeDtypeStruct
    vmem, anywhere = [
        pl.BlockSpec(memory_space=space) for space in (pltpu.VMEM, pl.ANY)
    ]
    sems = [(halves, 3, pieces)] * 4 + [(halves, pieces)] * 2
    return pl.pallas_call(
        functools.partial(layered_front_kernel, cycle, pieces),
        in_specs=[anywhere] * 4 + [vmem] * 4,
        out_specs=[vmem] * 4,
        out_shape=(
            shape((row_total, width), bf16),
            shape((width, row_total), bf16),
            shape((width, row_total), f32),
            shape((cycle, 2 * width // cycle + 16, width), bf16),
        ),
        scratch_shapes=[
            pltpu.VMEM((3, LANES, halves, row_total, half), bf16),
            pltpu.VMEM(dense.shape, bf16),
            pltpu.VMEM((halves, row_total, half), f32),
            pltpu.VMEM((halves, row_total, half), bf16),
            pltpu.VMEM((halves, row_total, half), bf16),
            pltpu.VMEM((2 * width + 8, width), f32),
            pltpu.SemaphoreType.DMA((halves, 3)),
            pltpu.SemaphoreType.DMA((step_count,)),
        ] + [pltpu.SemaphoreType.DMA(size) for size in sems for _ in range(2)],
        compiler_params=pltpu.CompilerParams(
            collective_id=4, has_side_effects=True, vmem_limit_bytes=36 * 2**20
        ),
        name="layered_front",
    )(features, behind, across, dense, weight_self, weight_neighbor, bias, cotangent)


def close_kernel(*refs):
    count = len(refs) // 2
    for source, target in zip(refs[:count], refs[count:]):
        target[...] = source[...]


def close(arrays):
    return pl.pallas_call(
        close_kernel,
        out_shape=tuple(jax.ShapeDtypeStruct(a.shape, a.dtype) for a in arrays),
        compiler_params=pltpu.CompilerParams(vmem_limit_bytes=8 * 2**20),
        name="close",
    )(*arrays)


def on_device(
    features,
    weight_self,
    weight_neighbor,
    bias_vector,
    tile_row,
    tile_column,
    tile_value,
    tile_count,
    tile_table,
    cotangent,
):
    f32, bf16 = jnp.float32, jnp.bfloat16
    cycle_length = lax.axis_size("blk")
    replicas = lax.axis_size("rep")
    step_count = cycle_length // replicas
    replica = lax.axis_index("rep")
    row_total, width = features.shape

    jump = jnp.minimum(replica, replicas - 1 - replica)
    jump_bits = max(replicas // 2 - 1, 0).bit_length()
    reverse = (2 * replica) // replicas

    def shifted(array, sign):
        for bit in range(jump_bits):
            by = sign * (step_count << bit)
            moved = jnp.where(
                reverse == 0,
                lax.ppermute(
                    array, "blk",
                    [(i, (i + by) % cycle_length) for i in range(cycle_length)],
                ),
                lax.ppermute(
                    array, "blk",
                    [(i, (i - by) % cycle_length) for i in range(cycle_length)],
                ),
            )
            array = jnp.where(jump // (1 << bit) % 2 == 1, moved, array)
        return array

    if is_layered(cycle_length, replicas):
        early = ahead_of_build(cycle_length, features)
    dense = build_dense(
        tile_row[0], tile_column[0], tile_value[0], tile_count[0], tile_table, row_total
    )
    if is_layered(cycle_length, replicas):
        activations, sent_t, self_t, grads = layered_front(
            cycle_length, features, *early, dense, weight_self, weight_neighbor,
            bias_vector.reshape(1, width), cotangent,
        )
        results = close((
            activations, *layered_backward(cycle_length, sent_t, self_t, dense, grads)
        ))
        return (*results[:4], results[4][0])
    mine = forward(cycle_length, replicas, shifted(features, 1), dense)
    bit = 1
    while True:
        other = lax.ppermute(mine, "rep", [(i, i ^ bit) for i in range(replicas)])
        bit *= 2
        if bit >= replicas:
            break
        mine = (mine.astype(f32) + other.astype(f32)).astype(bf16)
    activations, sent_t, self_t, grads = layer(
        cycle_length, features, mine, other, weight_self, weight_neighbor,
        bias_vector.reshape(1, width), cotangent,
    )
    pushed, part = backward(cycle_length, replicas, sent_t, dense, grads)
    pushed, part = shifted(pushed, -1), shifted(part, -1)

    def over_replicas(array):
        bit = 1
        while 2 * bit < replicas:
            other = lax.ppermute(array, "rep", [(i, i ^ bit) for i in range(replicas)])
            array = (array.astype(f32) + other.astype(f32)).astype(bf16)
            bit *= 2
        return array

    weights, bias_rows, grad_t = finish(
        cycle_length, replicas, over_replicas(pushed), over_replicas(part), self_t
    )
    weights = weights.reshape(2 * width, width)
    grad_features = grad_t.T
    return (
        activations,
        grad_features,
        weights[:width],
        weights[width:],
        bias_rows[0],
    )


def solution(mesh):
    placed = (
        P("blk", None),
        P(),
        P(),
        P(),
        P("blk", "rep", None),
        P("blk", "rep", None),
        P("blk", "rep", None),
        P("blk", "rep"),
        P(("blk", "rep"), None, None),
        P("blk", None),
    )
    return jax.shard_map(
        on_device,
        mesh=mesh,
        in_specs=placed,
        out_specs=(P("blk", None), P("blk", None), P(), P(), P()),
        check_vma=False,
    )
```

profile of v0, /device:TPU:0, one launch (start us, length us, event | category | flops | bytes accessed | tf_op | source)
XLA Modules:
  0.0 105.0 jit_solution(1284807054482745787)
XLA Ops:
  0.6 0.0 copy-start
  0.6 0.0 copy-start.2
  0.7 0.0 copy-start.3
  0.7 0.0 copy-start.4
  0.7 0.0 copy-start.1
  0.7 3.1 %collective-permute-start = (bf16[1024,256]{1,0:T(8,128)(2,1)}, bf16[1024,256]{1,0:T(8,128)(2,1)S(1)}, u32[]{:S(2)}, u32[]{:S(2)}) collective-permute-start(bf16[1024,256]{1,0:T(8,128)(2,1)} %features.1), channel_id=1, source_target_pairs={{0,8},{1,25},{2,10},{3,27},{4,12},{5,29},{6,14},{7,31},{8,16},{9,1... | collective-permute-start | bytes 1572872 | tf_op jit(solution)/shard_map/ppermute | solution.py:1187
  3.8 3.4 %collective-permute-start.1 = (bf16[1024,256]{1,0:T(8,128)(2,1)}, bf16[1024,256]{1,0:T(8,128)(2,1)S(1)}, u32[]{:S(2)}, u32[]{:S(2)}) collective-permute-start(bf16[1024,256]{1,0:T(8,128)(2,1)} %features.1), channel_id=1, source_target_pairs={{0,4},{2,6},{5,1},{7,3},{8,12},{10,14},{13,9},{15,11},{16,20},{18,... | collective-permute-start | bytes 1572872 | tf_op jit(solution)/shard_map/ppermute | solution.py:1187
  7.2 13.0 %build.1.dense = bf16[8,1024,1024]{2,1,0:T(8,128)(2,1)} custom-call(s32[8,64]{1,0:T(8,128)} %bitcast.7, s32[8,64]{1,0:T(8,128)} %bitcast.8, s32[8,64]{1,0:T(8,128)} %bitcast.9, s32[8]{0:T(128)} %bitcast.10, bf16[128,128,128]{2,1,0:T(8,128)(2,1)} %table.1), custom_call_target="tpu_custom_call" | custom-call | bytes 20971520 | tf_op jit(solution)/shard_map/build/pallas_call | solution.py:31
  20.2 0.0 collective-permute-done.behind
  20.2 0.0 collective-permute-done.1.across
  20.2 0.0 copy-done
  20.2 0.0 copy-done.2
  20.2 0.0 copy-done.3
  20.2 0.0 copy-done.4
  20.2 0.0 copy-done.1
  20.3 35.4 %layered_front.1 = (bf16[1024,256]{1,0:T(8,128)(2,1)S(1)}, bf16[256,1024]{1,0:T(8,128)(2,1)S(1)}, f32[256,1024]{1,0:T(8,128)S(1)}, bf16[16,48,256]{2,1,0:T(8,128)(2,1)S(1)}) custom-call(bf16[1024,256]{1,0:T(8,128)(2,1)S(1)} %copy-done, bf16[1024,256]{1,0:T(8,128)(2,1)S(1)} %collective-permute-done.behind, ...), custom_call_target="tpu_custom_call" | custom-call | tf_op jit(solution)/shard_map/layered_front/pallas_call | solution.py:1203
  55.7 48.1 %layered_backward.1 = (bf16[1024,256]{1,0:T(8,128)(2,1)S(1)}, f32[256,256]{1,0:T(8,128)S(1)}, f32[256,256]{1,0:T(8,128)S(1)}, f32[1,256]{1,0:T(1,128)S(1)}) custom-call(bf16[256,1024]{1,0:T(8,128)(2,1)S(1)} %get-tuple-element.19.sent_t, f32[256,1024]{1,0:T(8,128)S(1)} %get-tuple-element.20.self_t, bf16[8,1024,1024]{2,1,0:T(8,128)(2,1)} %build.1.dense, ...), custom_call_target="tpu_custom_call" | custom-call | tf_op jit(solution)/shard_map/layered_backward/pallas_call | solution.py:864
  103.7 1.2 %close.1 = (bf16[1024,256]{1,0:T(8,128)(2,1)}, bf16[1024,256]{1,0:T(8,128)(2,1)}, f32[256,256]{1,0:T(8,128)}, f32[256,256]{1,0:T(8,128)}, f32[1,256]{1,0:T(1,128)}) custom-call(bf16[1024,256]{1,0:T(8,128)(2,1)S(1)} %get-tuple-element.18.refs_0_, bf16[1024,256]{1,0:T(8,128)(2,1)S(1)} %get-tuple-element.22.refs_1_, f32[256,256]{1,0:T(8,128)S(1)} %get-tuple-element.23.refs_2_, ...), custom_call_target="tpu_custom_call" | custom-call | tf_op jit(solution)/shard_map/close/pallas_call | solution.py:1237
Async XLA Ops:
  0.6 19.6 %copy-start = (bf16[1024,256]{1,0:T(8,128)(2,1)S(1)}, bf16[1024,256]{1,0:T(8,128)(2,1)}, u32[]{:S(2)}) copy-start(bf16[1024,256]{1,0:T(8,128)(2,1)} %features.1) | copy-start | bytes 1572868
  0.6 19.6 %copy-start.2 = (bf16[256,256]{1,0:T(8,128)(2,1)S(1)}, bf16[256,256]{1,0:T(8,128)(2,1)}, u32[]{:S(2)}) copy-start(bf16[256,256]{1,0:T(8,128)(2,1)} %weight_self.1) | copy-start | bytes 393220
  0.7 19.6 %copy-start.3 = (bf16[256,256]{1,0:T(8,128)(2,1)S(1)}, bf16[256,256]{1,0:T(8,128)(2,1)}, u32[]{:S(2)}) copy-start(bf16[256,256]{1,0:T(8,128)(2,1)} %weight_neighbor.1) | copy-start | bytes 393220
  0.7 19.6 %copy-start.4 = (f32[256]{0:T(256)S(1)}, f32[256]{0:T(256)}, u32[]{:S(2)}) copy-start(f32[256]{0:T(256)} %param.13) | copy-start | bytes 3076
  0.7 19.6 %copy-start.1 = (bf16[1024,256]{1,0:T(8,128)(2,1)S(1)}, bf16[1024,256]{1,0:T(8,128)(2,1)}, u32[]{:S(2)}) copy-start(bf16[1024,256]{1,0:T(8,128)(2,1)} %cotangent.1) | copy-start | bytes 1572868
  0.7 19.5 %collective-permute-start = (bf16[1024,256]{1,0:T(8,128)(2,1)}, bf16[1024,256]{1,0:T(8,128)(2,1)S(1)}, u32[]{:S(2)}, u32[]{:S(2)}) collective-permute-start(bf16[1024,256]{1,0:T(8,128)(2,1)} %features.1), channel_id=1, source_target_pairs={{0,8},{1,25},{2,10},{3,27},{4,12},{5,29},{6,14},{7,31},{8,16},{9,1... | collective-permute-start | bytes 1572872 | tf_op jit(solution)/shard_map/ppermute | solution.py:1187
  3.8 16.4 %collective-permute-start.1 = (bf16[1024,256]{1,0:T(8,128)(2,1)}, bf16[1024,256]{1,0:T(8,128)(2,1)S(1)}, u32[]{:S(2)}, u32[]{:S(2)}) collective-permute-start(bf16[1024,256]{1,0:T(8,128)(2,1)} %features.1), channel_id=1, source_target_pairs={{0,4},{2,6},{5,1},{7,3},{8,12},{10,14},{13,9},{15,11},{16,20},{18,... | collective-permute-start | bytes 1572872 | tf_op jit(solution)/shard_map/ppermute | solution.py:1187
where the time goes:
time: 106 us; the launch traced here: 105 us
  Pallas kernels  97.7 us (92%)
  starting transfers between devices  6.55 us (6%)
    pallas_call x1, Pallas kernels, layered_backward(): pl.pallas_call(functools.partial(layered_backward_kernel, cycle, pieces),...  48.1 us
    pallas_call x1, Pallas kernels, layered_front(): pl.pallas_call(functools.partial(layered_front_kernel, cycle, pieces), in...  35.4 us
    pallas_call x1, Pallas kernels, build_dense(): pl.pallas_call(build_kernel, grid_spec=pltpu.PrefetchScalarGridSpec(num_s...  13 us
    ppermute x2, starting transfers between devices, ahead_of_build(): lax.ppermute(features, ('blk', 'rep'), pairs)  6.55 us
  transfers between devices with their start and end apart: 2, of which 0 were waited for; matrix products, arithmetic and copies ran while one was open for 0% of the time, Pallas kernels for 12%

commit v1 on v0

--- a/solution.py
+++ b/solution.py
@@ -495,13 +495,12 @@
     )
 
 
-def layered_backward_kernel(
-    cycle, pieces, sent_t, self_t, dense, grads,
+def backward_part(
+    cycle, pieces, weight_self, sent_t, grad_pre, blocks, grads, fill_grads,
     grad_out, weight_self_out, weight_neighbor_out, bias_out,
-    blocks, acc, core_out, core_in, pair_out, pair_in, layer_out, layer_in,
+    acc, core_out, core_in, pair_out, pair_in, layer_out, layer_in,
     rep_out, rep_in, far_out, far_in, part_acc, core_part, pair_part_out, pair_part,
-    layer_part_out, layer_part, rep_part_out, rep_part, gathered, block_sem,
-    *sems,
+    layer_part_out, layer_part, rep_part_out, rep_part, gathered, *sems,
 ):
     f32 = jnp.float32
     bf16 = jnp.bfloat16
@@ -514,20 +513,9 @@
      layer_part_sems, rep_part_sems, spread_sems, widen_sems, far_sems) = [
         (sems[2 * k], sems[2 * k + 1]) for k in range(11)
     ]
-    by_layer = pieces // 2
+    by_layer = 1
     partner = {"rep": 1 - at.replica}
     onward = {"blk": at.at_layer(-at.sign)}
-
-    def load(step):
-        return pltpu.make_async_copy(
-            dense.at[step], blocks.at[step], block_sem.at[step]
-        )
-
-    @pl.loop(0, steps)
-    def _(hop):
-        load((steps - 1 - hop) * (1 - at.replica) + hop * at.replica).start()
-
-    at.greet()
 
     def own_lane(side):
         return 2 * side + at.core
@@ -620,11 +608,6 @@
 
     def product(i, d, n, lane, store):
         step = at.step(at.lane, lane, d)
-
-        @pl.when(n == 0)
-        def _():
-            load(step).wait()
-
         wide = pl.ds(pl.multiple_of(n * size, 2 * size), 2 * size)
         value = jnp.dot(
             sent_t[...], blocks[step, :, wide], preferred_element_type=f32
@@ -710,6 +693,7 @@
                 close(n - 1)
 
     def parts_to_core():
+        fill_grads()
         for d in range(3):
             for side in range(2):
                 pl.when(sends_core(d, side))(
@@ -775,14 +759,15 @@
 
     def close(n):
         rep_copy(n).wait_recv()
-        total = (
-            self_t[:, span(n)] + rep_out[n].astype(f32) + rep_in[n].astype(f32)
-        )
-        grad_out[span(n), :] = total.T.astype(grad_out.dtype)
+        pushed = rep_out[n].astype(f32) + rep_in[n].astype(f32)
+        own = lax.dot_general(
+            grad_pre[span(n), :], weight_self[...], COLS_COLS, preferred_element_type=f32
+        )
+        grad_out[span(n), :] = (own + pushed.T).astype(grad_out.dtype)
 
     timetable = (
-        (0, parts_to_core),
-        (2, parts_to_pair),
+        (1, parts_to_core),
+        (3, parts_to_pair),
         (pieces + 2, functools.partial(part_onward, 2)),
         (2 * pieces + 1, functools.partial(part_onward, 1)),
         (2 * pieces + 3, functools.partial(part_onward, 0)),
@@ -793,17 +778,17 @@
 
     @pl.loop(0, 4 * pieces)
     def _(i):
+        @pl.when(jnp.logical_and(i > 0, i <= 3 * pieces))
+        def _():
+            over_pair(i - 1)
+
+        @pl.when(i >= pieces)
+        def _():
+            over_layers(i - pieces)
+
         @pl.when(jnp.logical_and(i < 3 * pieces, lax.rem(i, 2) == 0))
         def _():
             begin(i)
-
-        @pl.when(jnp.logical_and(i > 0, i <= 3 * pieces))
-        def _():
-            over_pair(i - 1)
-
-        @pl.when(i >= pieces)
-        def _():
-            over_layers(i - pieces)
 
         for turn, act in timetable:
             pl.when(i == turn)(act)
@@ -846,12 +831,8 @@
         widen(k).wait_send()
 
 
-def layered_backward(cycle, sent_t, self_t, dense, grads):
-    step_count, row_total, _ = dense.shape
-    width = sent_t.shape[0]
-    part = grads.shape[1:]
+def backward_scratch(cycle, pieces, row_total, width, part):
     depth = 2 * width // cycle
-    pieces = 4
     panel = (width, row_total // pieces)
     bf16, f32 = jnp.bfloat16, jnp.float32
     layers = cycle // LANES
@@ -860,54 +841,36 @@
         (turns, 2), (turns,), (2 * pieces,), (pieces,), (3, 2), (3,), (2,), (1,),
         (layers,), (3,), (pieces // 2,),
     ]
-    vmem = pl.BlockSpec(memory_space=pltpu.VMEM)
-    return pl.pallas_call(
-        functools.partial(layered_backward_kernel, cycle, pieces),
-        in_specs=[vmem, vmem, pl.BlockSpec(memory_space=pl.ANY), vmem],
-        out_specs=[vmem] * 4,
-        out_shape=(
-            jax.ShapeDtypeStruct((row_total, width), bf16),
-            jax.ShapeDtypeStruct((width, width), f32),
-            jax.ShapeDtypeStruct((width, width), f32),
-            jax.ShapeDtypeStruct((1, width), f32),
-        ),
-        scratch_shapes=[
-            pltpu.VMEM(dense.shape, bf16),
-            pltpu.VMEM((turns, 2, *panel), f32),
-            pltpu.VMEM((turns, 2, *panel), bf16),
-            pltpu.VMEM((turns, 2, *panel), bf16),
-            pltpu.VMEM((turns, *panel), bf16),
-            pltpu.VMEM((turns, *panel), bf16),
-            pltpu.VMEM((2 * pieces, *panel), bf16),
-            pltpu.VMEM((2 * pieces, *panel), bf16),
-            pltpu.VMEM((pieces, *panel), bf16),
-            pltpu.VMEM((pieces, *panel), bf16),
-            pltpu.VMEM((pieces // 2, *panel), bf16),
-            pltpu.VMEM((pieces // 2, *panel), bf16),
-            pltpu.VMEM((3, 2, *part), f32),
-            pltpu.VMEM((3, 2, *part), bf16),
-            pltpu.VMEM((3, *part), bf16),
-            pltpu.VMEM((3, *part), bf16),
-            pltpu.VMEM((2, *part), bf16),
-            pltpu.VMEM((2, *part), bf16),
-            pltpu.VMEM(part, bf16),
-            pltpu.VMEM(part, bf16),
-            pltpu.VMEM((LANES, layers, depth, width), bf16),
-            pltpu.SemaphoreType.DMA((step_count,)),
-        ] + [pltpu.SemaphoreType.DMA(shape) for shape in sems for _ in range(2)],
-        compiler_params=pltpu.CompilerParams(
-            collective_id=3, has_side_effects=True, vmem_limit_bytes=44 * 2**20
-        ),
-        name="layered_backward",
-    )(sent_t, self_t, dense, grads)
-
-
-def layered_front_kernel(
-    cycle, pieces, features, behind, across, dense,
+    both = [
+        ((turns, 2, *panel), bf16), ((turns, *panel), bf16),
+        ((2 * pieces, *panel), bf16), ((pieces, *panel), bf16),
+        ((pieces // 2, *panel), bf16),
+    ]
+    return [
+        pltpu.VMEM((turns, 2, *panel), f32),
+    ] + [
+        pltpu.VMEM(*buffer) for buffer in both for _ in range(2)
+    ] + [
+        pltpu.VMEM((3, 2, *part), f32),
+        pltpu.VMEM((3, 2, *part), bf16),
+        pltpu.VMEM((3, *part), bf16),
+        pltpu.VMEM((3, *part), bf16),
+        pltpu.VMEM((2, *part), bf16),
+        pltpu.VMEM((2, *part), bf16),
+        pltpu.VMEM(part, bf16),
+        pltpu.VMEM(part, bf16),
+        pltpu.VMEM((LANES, layers, depth, width), bf16),
+    ] + [pltpu.SemaphoreType.DMA(shape) for shape in sems for _ in range(2)]
+
+
+def layered_kernel(
+    cycle, pieces, back_pieces, features, behind, across, dense,
     weight_self, weight_neighbor, bias, cotangent,
-    activations, sent_t, self_t, grads,
-    slots, blocks, total, rep_out, rep_in, sums, first_sem, block_sem, *sems,
+    activations, grad_out, weight_self_out, weight_neighbor_out, bias_out,
+    sent_t, grad_store, aggregate_store, grads,
+    slots, blocks, total, rep_out, rep_in, first_sem, block_sem, *rest,
 ):
+    sems, back = rest[:12], rest[12:]
     f32, bf16 = jnp.float32, jnp.bfloat16
     steps, rows = blocks.shape[0], blocks.shape[1]
     halves, half = total.shape[0], total.shape[2]
@@ -1088,7 +1051,6 @@
         give_all(h, 0, ("core",))
         relay(h, 0)
     total[...] = jnp.zeros_like(total)
-    sums[...] = jnp.zeros_like(sums)
     whole(0, 0)
     relay(0, 1, lambda p: give(1, 1, p, ("pair", "core")))
     give_all(1, 1, ("layer",))
@@ -1106,7 +1068,8 @@
     def joined(ref, place):
         return jnp.concatenate([ref[h, place] for h in range(halves)], axis=1)
 
-    width = halves * half
+    def own_rows(place):
+        return jnp.concatenate([slots[0, lane, h, place] for h in range(halves)], axis=1)
 
     @pl.loop(0, pieces)
     def _(p):
@@ -1115,11 +1078,9 @@
             rep_copy(h, p).wait_recv()
         mine, other = joined(rep_out, place), joined(rep_in, place)
         aggregate = (mine.astype(f32) + other.astype(f32)).astype(bf16)
-        own_rows = jnp.concatenate(
-            [slots[0, lane, h, place] for h in range(halves)], axis=1
-        )
+        aggregate_store[place, :] = aggregate
         pre = (
-            jnp.dot(own_rows, weight_self[...], preferred_element_type=f32)
+            jnp.dot(own_rows(place), weight_self[...], preferred_element_type=f32)
             + jnp.dot(aggregate, weight_neighbor[...], preferred_element_type=f32)
             + bias[...]
         )
@@ -1127,33 +1088,35 @@
         activations[place, :] = (pre * sigmoid).astype(activations.dtype)
         derivative = sigmoid * (1.0 + pre * (1.0 - sigmoid))
         grad_pre = (cotangent[place, :].astype(f32) * derivative).astype(bf16)
+        grad_store[place, :] = grad_pre
         sent_t[:, place] = lax.dot_general(
             weight_neighbor[...], grad_pre, COLS_COLS, preferred_element_type=f32
         ).astype(sent_t.dtype)
-        self_t[:, place] = lax.dot_general(
-            weight_self[...], grad_pre, COLS_COLS, preferred_element_type=f32
-        )
-        sums[0:width] += lax.dot_general(
-            own_rows, grad_pre, ROWS_ROWS, preferred_element_type=f32
-        )
-        sums[width : 2 * width] += lax.dot_general(
-            aggregate, grad_pre, ROWS_ROWS, preferred_element_type=f32
-        )
-        sums[2 * width : 2 * width + 1] += jnp.sum(
-            grad_pre.astype(f32), axis=0, keepdims=True
-        )
-
+
+    width = halves * half
     parts = grads.shape[0]
     depth = 2 * width // parts
-    tail = grads.shape[1] - depth
-    bias_rows = jnp.broadcast_to(
-        sums[2 * width : 2 * width + 1], (tail, width)
-    ).astype(grads.dtype)
-    for part in range(parts):
-        grads[part, 0:depth, :] = sums[part * depth : (part + 1) * depth].astype(
-            grads.dtype
-        )
-        grads[part, depth:, :] = bias_rows
+
+    def fill_grads():
+        grad_pre = grad_store[...]
+        summed = jnp.sum(grad_pre.astype(f32), axis=0, keepdims=True)
+        bias_rows = jnp.broadcast_to(
+            summed, (grads.shape[1] - depth, width)
+        ).astype(grads.dtype)
+        for k in range(2):
+            value = lax.dot_general(
+                own_rows(slice(None)) if k == 0 else aggregate_store[...],
+                grad_pre, ROWS_ROWS, preferred_element_type=f32,
+            ).astype(grads.dtype)
+            for part in range(parts // 2):
+                rows_of = slice(part * depth, (part + 1) * depth)
+                grads[k * (parts // 2) + part, 0:depth, :] = value[rows_of]
+                grads[k * (parts // 2) + part, depth:, :] = bias_rows
+
+    backward_part(
+        cycle, back_pieces, weight_self, sent_t, grad_store, blocks, grads, fill_grads,
+        grad_out, weight_self_out, weight_neighbor_out, bias_out, *back,
+    )
 
     @pl.loop(0, pieces)
     def _(p):
@@ -1187,13 +1150,14 @@
     return [lax.ppermute(features, ("blk", "rep"), pairs) for pairs in (behind, across)]
 
 
-def layered_front(
+def layered(
     cycle, features, behind, across, dense, weight_self, weight_neighbor, bias, cotangent
 ):
     step_count, row_total, _ = dense.shape
     width = features.shape[1]
-    pieces, halves = 4, 2
+    pieces, back_pieces, halves = 4, 4, 2
     half = width // halves
+    part = (2 * width // cycle + 16, width)
     bf16, f32 = jnp.bfloat16, jnp.float32
     shape = jax.ShapeDtypeStruct
     vmem, anywhere = [
@@ -1201,29 +1165,35 @@
     ]
     sems = [(halves, 3, pieces)] * 4 + [(halves, pieces)] * 2
     return pl.pallas_call(
-        functools.partial(layered_front_kernel, cycle, pieces),
+        functools.partial(layered_kernel, cycle, pieces, back_pieces),
         in_specs=[anywhere] * 4 + [vmem] * 4,
-        out_specs=[vmem] * 4,
+        out_specs=[vmem] * 5,
         out_shape=(
             shape((row_total, width), bf16),
-            shape((width, row_total), bf16),
-            shape((width, row_total), f32),
-            shape((cycle, 2 * width // cycle + 16, width), bf16),
+            shape((row_total, width), bf16),
+            shape((width, width), f32),
+            shape((width, width), f32),
+            shape((1, width), f32),
         ),
         scratch_shapes=[
+            pltpu.VMEM((width, row_total), bf16),
+            pltpu.VMEM((row_total, width), bf16),
+            pltpu.VMEM((row_total, width), bf16),
+            pltpu.VMEM((cycle, *part), bf16),
             pltpu.VMEM((3, LANES, halves, row_total, half), bf16),
             pltpu.VMEM(dense.shape, bf16),
             pltpu.VMEM((halves, row_total, half), f32),
             pltpu.VMEM((halves, row_total, half), bf16),
             pltpu.VMEM((halves, row_total, half), bf16),
-            pltpu.VMEM((2 * width + 8, width), f32),
             pltpu.SemaphoreType.DMA((halves, 3)),
             pltpu.SemaphoreType.DMA((step_count,)),
-        ] + [pltpu.SemaphoreType.DMA(size) for size in sems for _ in range(2)],
+        ]
+        + [pltpu.SemaphoreType.DMA(size) for size in sems for _ in range(2)]
+        + backward_scratch(cycle, back_pieces, row_total, width, part),
         compiler_params=pltpu.CompilerParams(
-            collective_id=4, has_side_effects=True, vmem_limit_bytes=36 * 2**20
+            collective_id=3, has_side_effects=True, vmem_limit_bytes=47 * 2**20
         ),
-        name="layered_front",
+        name="layered",
     )(features, behind, across, dense, weight_self, weight_neighbor, bias, cotangent)
 
 
@@ -1288,12 +1258,9 @@
         tile_row[0], tile_column[0], tile_value[0], tile_count[0], tile_table, row_total
     )
     if is_layered(cycle_length, replicas):
-        activations, sent_t, self_t, grads = layered_front(
+        results = close(layered(
             cycle_length, features, *early, dense, weight_self, weight_neighbor,
             bias_vector.reshape(1, width), cotangent,
-        )
-        results = close((
-            activations, *layered_backward(cycle_length, sent_t, self_t, dense, grads)
         ))
         return (*results[:4], results[4][0])
     mine = forward(cycle_length, replicas, shifted(features, 1), dense)

time: 106 us -> 99.3 us (0.937)
  Pallas kernels: 97.7 us -> 91.3 us
    pallas_call x2 -> x1, Pallas kernels: 83.5 us -> 77.2 us  [layered(): pl.pallas_call(functools.partial(layered_kernel, cycle, pieces, back_piec...]
  transfers between devices with their start and end apart: 2 -> 2, of which waited for: 0 -> 0; matrix products, arithmetic and copies ran while one was open for 0% -> 0% of each run, Pallas kernels for 12% -> 13%
where the time goes in v1:
time: 99.3 us; the launch traced here: 98.6 us
  Pallas kernels  91.3 us (92%)
  starting transfers between devices  6.55 us (7%)
    pallas_call x1, Pallas kernels, layered(): pl.pallas_call(functools.partial(layered_kernel, cycle, pieces, back_piec...  77.2 us
    pallas_call x1, Pallas kernels, build_dense(): pl.pallas_call(build_kernel, grid_spec=pltpu.PrefetchScalarGridSpec(num_s...  12.8 us
    ppermute x2, starting transfers between devices, ahead_of_build(): lax.ppermute(features, ('blk', 'rep'), pairs)  6.55 us
  transfers between devices with their start and end apart: 2, of which 0 were waited for; matrix products, arithmetic and copies ran while one was open for 0% of the time, Pallas kernels for 13%

profile of v1, /device:TPU:0, one launch (start us, length us, event | category | flops | bytes accessed | tf_op | source)
XLA Modules:
  0.0 98.6 jit_solution(9800955618906145738)
XLA Ops:
  0.6 0.0 copy-start
  0.6 0.0 copy-start.1
  0.7 0.0 copy-start.4
  0.7 0.0 copy-start.3
  0.7 0.0 copy-start.2
  0.7 3.1 %collective-permute-start = (bf16[1024,256]{1,0:T(8,128)(2,1)}, bf16[1024,256]{1,0:T(8,128)(2,1)S(1)}, u32[]{:S(2)}, u32[]{:S(2)}) collective-permute-start(bf16[1024,256]{1,0:T(8,128)(2,1)} %features.1), channel_id=1, source_target_pairs={{0,8},{1,25},{2,10},{3,27},{4,12},{5,29},{6,14},{7,31},{8,16},{9,1... | collective-permute-start | bytes 1572872 | tf_op jit(solution)/shard_map/ppermute | solution.py:1150
  3.8 3.4 %collective-permute-start.1 = (bf16[1024,256]{1,0:T(8,128)(2,1)}, bf16[1024,256]{1,0:T(8,128)(2,1)S(1)}, u32[]{:S(2)}, u32[]{:S(2)}) collective-permute-start(bf16[1024,256]{1,0:T(8,128)(2,1)} %features.1), channel_id=1, source_target_pairs={{0,4},{2,6},{5,1},{7,3},{8,12},{10,14},{13,9},{15,11},{16,20},{18,... | collective-permute-start | bytes 1572872 | tf_op jit(solution)/shard_map/ppermute | solution.py:1150
  7.2 12.8 %build.1.dense = bf16[8,1024,1024]{2,1,0:T(8,128)(2,1)} custom-call(s32[8,64]{1,0:T(8,128)} %bitcast.7, s32[8,64]{1,0:T(8,128)} %bitcast.8, s32[8,64]{1,0:T(8,128)} %bitcast.9, s32[8]{0:T(128)} %bitcast.10, bf16[128,128,128]{2,1,0:T(8,128)(2,1)} %table.1), custom_call_target="tpu_custom_call" | custom-call | bytes 20971520 | tf_op jit(solution)/shard_map/build/pallas_call | solution.py:31
  20.1 0.0 collective-permute-done.behind
  20.1 0.0 collective-permute-done.1.across
  20.1 0.0 copy-done
  20.1 0.0 copy-done.1
  20.1 0.0 copy-done.4
  20.1 0.0 copy-done.3
  20.1 0.0 copy-done.2
  20.1 77.2 %layered.1 = (bf16[1024,256]{1,0:T(8,128)(2,1)S(1)}, bf16[1024,256]{1,0:T(8,128)(2,1)S(1)}, f32[256,256]{1,0:T(8,128)S(1)}, f32[256,256]{1,0:T(8,128)S(1)}, f32[1,256]{1,0:T(1,128)S(1)}) custom-call(bf16[1024,256]{1,0:T(8,128)(2,1)S(1)} %copy-done, bf16[1024,256]{1,0:T(8,128)(2,1)S(1)} %collective-permute-done.behind, ...), custom_call_target="tpu_custom_call" | custom-call | tf_op jit(solution)/shard_map/layered/pallas_call | solution.py:1167
  97.3 1.2 %close.1 = (bf16[1024,256]{1,0:T(8,128)(2,1)}, bf16[1024,256]{1,0:T(8,128)(2,1)}, f32[256,256]{1,0:T(8,128)}, f32[256,256]{1,0:T(8,128)}, f32[1,256]{1,0:T(1,128)}) custom-call(bf16[1024,256]{1,0:T(8,128)(2,1)S(1)} %get-tuple-element.15.refs_0_, bf16[1024,256]{1,0:T(8,128)(2,1)S(1)} %get-tuple-element.16.refs_1_, f32[256,256]{1,0:T(8,128)S(1)} %get-tuple-element.17.refs_2_, ...), custom_call_target="tpu_custom_call" | custom-call | tf_op jit(solution)/shard_map/close/pallas_call | solution.py:1207
Async XLA Ops:
  0.6 19.5 %copy-start = (bf16[1024,256]{1,0:T(8,128)(2,1)S(1)}, bf16[1024,256]{1,0:T(8,128)(2,1)}, u32[]{:S(2)}) copy-start(bf16[1024,256]{1,0:T(8,128)(2,1)} %features.1) | copy-start | bytes 1572868
  0.6 19.4 %copy-start.1 = (bf16[1024,256]{1,0:T(8,128)(2,1)S(1)}, bf16[1024,256]{1,0:T(8,128)(2,1)}, u32[]{:S(2)}) copy-start(bf16[1024,256]{1,0:T(8,128)(2,1)} %cotangent.1) | copy-start | bytes 1572868
  0.7 19.4 %copy-start.4 = (f32[256]{0:T(256)S(1)}, f32[256]{0:T(256)}, u32[]{:S(2)}) copy-start(f32[256]{0:T(256)} %param.13) | copy-start | bytes 3076
  0.7 19.4 %copy-start.3 = (bf16[256,256]{1,0:T(8,128)(2,1)S(1)}, bf16[256,256]{1,0:T(8,128)(2,1)}, u32[]{:S(2)}) copy-start(bf16[256,256]{1,0:T(8,128)(2,1)} %weight_neighbor.1) | copy-start | bytes 393220
  0.7 19.4 %copy-start.2 = (bf16[256,256]{1,0:T(8,128)(2,1)S(1)}, bf16[256,256]{1,0:T(8,128)(2,1)}, u32[]{:S(2)}) copy-start(bf16[256,256]{1,0:T(8,128)(2,1)} %weight_self.1) | copy-start | bytes 393220
  0.7 19.4 %collective-permute-start = (bf16[1024,256]{1,0:T(8,128)(2,1)}, bf16[1024,256]{1,0:T(8,128)(2,1)S(1)}, u32[]{:S(2)}, u32[]{:S(2)}) collective-permute-start(bf16[1024,256]{1,0:T(8,128)(2,1)} %features.1), channel_id=1, source_target_pairs={{0,8},{1,25},{2,10},{3,27},{4,12},{5,29},{6,14},{7,31},{8,16},{9,1... | collective-permute-start | bytes 1572872 | tf_op jit(solution)/shard_map/ppermute | solution.py:1150
  3.8 16.3 %collective-permute-start.1 = (bf16[1024,256]{1,0:T(8,128)(2,1)}, bf16[1024,256]{1,0:T(8,128)(2,1)S(1)}, u32[]{:S(2)}, u32[]{:S(2)}) collective-permute-start(bf16[1024,256]{1,0:T(8,128)(2,1)} %features.1), channel_id=1, source_target_pairs={{0,4},{2,6},{5,1},{7,3},{8,12},{10,14},{13,9},{15,11},{16,20},{18,... | collective-permute-start | bytes 1572872 | tf_op jit(solution)/shard_map/ppermute | solution.py:1150

commit v2 on v1

--- a/solution.py
+++ b/solution.py
@@ -513,7 +513,8 @@
      layer_part_sems, rep_part_sems, spread_sems, widen_sems, far_sems) = [
         (sems[2 * k], sems[2 * k + 1]) for k in range(11)
     ]
-    by_layer = 1
+    by_layer = pieces // 4
+    group = pieces // 2
     partner = {"rep": 1 - at.replica}
     onward = {"blk": at.at_layer(-at.sign)}
 
@@ -570,53 +571,56 @@
         return remote(gathered.at[lane], gathered.at[lane], widen_sems, k,
                       {"blk": device})
 
+    core_sends = [[at.meets(at.lane, other_lane(k), d) for k in range(2)] for d in range(3)]
+    core_gets = [
+        [at.meets(at.lane_beside, own_lane(k), d) for k in range(2)] for d in range(3)
+    ]
+    owns = [[at.meets(at.lane, own_lane(k), d) for k in range(2)] for d in range(3)]
+    pair_sends = [at.chip_meets(at.pair, at.lane_across, d) for d in range(3)]
+    pair_gets = [at.chip_meets(1 - at.pair, at.lane, d) for d in range(3)]
+    chip_far = at.chip_meets(at.pair, at.lane, 2)
+    layer_far = at.layer_meets(at.lane, 2)
+
+    def sends_far(n):
+        return jnp.logical_and(n < by_layer, pair_sends[2])
+
     def sends_core(d, side):
-        return at.meets(at.lane, other_lane(side), d)
+        return core_sends[d][side]
 
     def gets_core(d, side):
-        return at.meets(at.lane_beside, own_lane(side), d)
-
-    def early(d, n):
-        return jnp.logical_and(d == 2, n < by_layer)
-
-    def sends_far(n):
-        return jnp.logical_and(n < by_layer, at.chip_meets(at.pair, at.lane_across, 2))
+        return core_gets[d][side]
+
+    def late(here, d, n):
+        return here if d < 2 or n is None else jnp.logical_and(here, n >= by_layer)
 
     def sends_pair(d, n=None):
-        here = at.chip_meets(at.pair, at.lane_across, d)
+        return late(pair_sends[d], d, n)
+
+    def gets_pair(d, n=None):
+        return late(pair_gets[d], d, n)
+
+    def sends_layer(d, n=None):
+        if d < 2:
+            return True
         if n is None:
-            return here
-        return jnp.logical_and(here, jnp.logical_not(early(d, n)))
-
-    def gets_pair(d, n=None):
-        there = at.chip_meets(1 - at.pair, at.lane, d)
-        if n is None:
-            return there
-        return jnp.logical_and(there, jnp.logical_not(early(d, n)))
-
-    def sends_layer(d, n=None):
-        far = at.layer_meets(at.lane, 2)
-        if n is not None:
-            far = jnp.logical_or(
-                at.chip_meets(at.pair, at.lane, 2),
-                jnp.logical_and(far, n >= by_layer),
-            )
-        return jnp.logical_and(d > 0, jnp.logical_or(d == 1, far))
-
-    def gets_layer(d, n):
-        return jnp.logical_and(d < 2, sends_layer(d + 1, n))
+            return layer_far
+        return jnp.logical_or(chip_far, jnp.logical_and(layer_far, n >= by_layer))
+
+    def when(condition):
+        return (lambda act: act()) if condition is True else pl.when(condition)
 
     def product(i, d, n, lane, store):
         step = at.step(at.lane, lane, d)
-        wide = pl.ds(pl.multiple_of(n * size, 2 * size), 2 * size)
+        width = group * size
+        wide = pl.ds(pl.multiple_of(n * size, width), width)
         value = jnp.dot(
             sent_t[...], blocks[step, :, wide], preferred_element_type=f32
         )
-        store(i, value[:, :size])
-        store(i + 1, value[:, size:])
-
-    def begin(i):
-        d, n = 2 - i // pieces, lax.rem(i, pieces)
+        for k in range(group):
+            store(i + k, value[:, k * size : (k + 1) * size])
+
+    def begin(d, n):
+        i = (2 - d) * pieces + n
         for side in range(2):
             @pl.when(sends_core(d, side))
             def _():
@@ -624,11 +628,11 @@
                     core_out[i, side] = value.astype(bf16)
 
                 product(i, d, n, other_lane(side), store)
-                core_copy(i, side).start()
-                core_copy(i + 1, side).start()
+                for k in range(group):
+                    core_copy(i + k, side).start()
 
         for side in range(2):
-            own = at.meets(at.lane, own_lane(side), d)
+            own = owns[d][side]
 
             @pl.when(own)
             def _():
@@ -639,52 +643,52 @@
 
             @pl.when(jnp.logical_not(own))
             def _():
-                for k in range(2):
+                for k in range(group):
                     acc[i + k, side] = jnp.zeros(acc.shape[2:], f32)
 
-    def over_pair(i):
-        d, n = 2 - i // pieces, lax.rem(i, pieces)
+    def over_pair(d, n):
+        i = (2 - d) * pieces + n
         for side in range(2):
             @pl.when(gets_core(d, side))
             def _():
                 core_copy(i, side).wait_recv()
                 acc[i, side] += core_in[i, side].astype(f32)
 
-        @pl.when(jnp.logical_and(d == 2, sends_far(n)))
-        def _():
-            far_out[n] = acc[i, 1 - at.pair].astype(bf16)
-            far_copy(n).start()
-
-        @pl.when(jnp.logical_and(d == 1, sends_far(n)))
-        def _():
-            far_copy(n).wait_recv()
-            acc[i, 1 - at.pair] += far_in[n].astype(f32)
+        if d > 0:
+            @pl.when(sends_far(n))
+            def _():
+                if d == 2:
+                    far_out[n] = acc[i, 1 - at.pair].astype(bf16)
+                    far_copy(n).start()
+                else:
+                    far_copy(n).wait_recv()
+                    acc[i, 1 - at.pair] += far_in[n].astype(f32)
 
         @pl.when(sends_pair(d, n))
         def _():
             pair_out[i] = acc[i, 1 - at.pair].astype(bf16)
             pair_copy(i).start()
 
-    def over_layers(i):
-        d, n = 2 - i // pieces, lax.rem(i, pieces)
+    def over_layers(d, n):
+        i = (2 - d) * pieces + n
 
         @pl.when(gets_pair(d, n))
         def _():
             pair_copy(i).wait_recv()
             acc[i, at.pair] += pair_in[i].astype(f32)
 
-        @pl.when(gets_layer(d, n))
-        def _():
-            layer_copy(i - pieces).wait_recv()
-            acc[i, at.pair] += layer_in[i - pieces].astype(f32)
-
-        @pl.when(sends_layer(d, n))
-        def _():
-            layer_out[i] = acc[i, at.pair].astype(bf16)
-            layer_copy(i).start()
-
-        @pl.when(d == 0)
-        def _():
+        if d < 2:
+            @when(sends_layer(d + 1, n))
+            def _():
+                layer_copy(i - pieces).wait_recv()
+                acc[i, at.pair] += layer_in[i - pieces].astype(f32)
+
+        if d > 0:
+            @when(sends_layer(d, n))
+            def _():
+                layer_out[i] = acc[i, at.pair].astype(bf16)
+                layer_copy(i).start()
+        else:
             rep_out[n] = acc[i, at.pair].astype(bf16)
             rep_copy(n).start()
 
@@ -703,7 +707,7 @@
     def parts_to_pair():
         for d in range(3):
             for side in range(2):
-                own = at.meets(at.lane, own_lane(side), d)
+                own = owns[d][side]
                 part_acc[d, side] = grads[part_of(d, own_lane(side))].astype(
                     f32
                 ) * own.astype(f32)
@@ -725,13 +729,13 @@
             part_acc[d, at.pair] += pair_part[d].astype(f32)
 
         if d < 2:
-            @pl.when(sends_layer(d + 1))
+            @when(sends_layer(d + 1))
             def _():
                 layer_part_copy(d + 1).wait_recv()
                 part_acc[d, at.pair] += layer_part[d].astype(f32)
 
         if d > 0:
-            @pl.when(sends_layer(d))
+            @when(sends_layer(d))
             def _():
                 layer_part_out[d - 1] = part_acc[d, at.pair].astype(bf16)
                 layer_part_copy(d).start()
@@ -765,33 +769,33 @@
         )
         grad_out[span(n), :] = (own + pushed.T).astype(grad_out.dtype)
 
+    quarter = pieces // 4
     timetable = (
-        (1, parts_to_core),
-        (3, parts_to_pair),
-        (pieces + 2, functools.partial(part_onward, 2)),
-        (2 * pieces + 1, functools.partial(part_onward, 1)),
-        (2 * pieces + 3, functools.partial(part_onward, 0)),
+        (2 * quarter, parts_to_core),
+        (pieces, parts_to_pair),
+        (pieces + 2 * quarter, functools.partial(part_onward, 2)),
+        (2 * pieces + quarter, functools.partial(part_onward, 1)),
+        (2 * pieces + 3 * quarter, functools.partial(part_onward, 0)),
         (3 * pieces, part_spread),
-        (3 * pieces + 2, part_over_pair),
-        (3 * pieces + 3, part_over_core),
+        (3 * pieces + 2 * quarter, part_over_pair),
+        (3 * pieces + 3 * quarter, part_over_core),
     )
 
-    @pl.loop(0, 4 * pieces)
-    def _(i):
-        @pl.when(jnp.logical_and(i > 0, i <= 3 * pieces))
-        def _():
-            over_pair(i - 1)
-
-        @pl.when(i >= pieces)
-        def _():
-            over_layers(i - pieces)
-
-        @pl.when(jnp.logical_and(i < 3 * pieces, lax.rem(i, 2) == 0))
-        def _():
-            begin(i)
-
-        for turn, act in timetable:
-            pl.when(i == turn)(act)
+    for d in (2, 1, 0, -1):
+        if d < 2:
+            over_pair(d + 1, pieces - 1)
+
+        @pl.loop(0, pieces)
+        def _(n):
+            if d >= 0:
+                pl.when(n > 0)(lambda: over_pair(d, n - 1))
+            if d < 2:
+                over_layers(d + 1, n)
+            if d >= 0:
+                pl.when(lax.rem(n, group) == 0)(lambda: begin(d, n))
+            for turn, act in timetable:
+                if turn // pieces == 2 - d:
+                    pl.when(n == turn % pieces)(act)
 
     widen(1).wait_recv()
     widen(2).wait_recv()
@@ -804,26 +808,24 @@
             out[place : place + depth, :] = gathered[lane, layer].astype(f32)
     close(pieces - 1)
 
-    @pl.loop(0, 3 * pieces)
-    def _(i):
-        d, n = 2 - i // pieces, lax.rem(i, pieces)
-
-        for side in range(2):
-            pl.when(sends_core(d, side))(lambda: core_copy(i, side).wait_send())
-        pl.when(sends_pair(d, n))(lambda: pair_copy(i).wait_send())
-        pl.when(sends_layer(d, n))(lambda: layer_copy(i).wait_send())
-
-        @pl.when(d == 0)
-        def _():
-            rep_copy(n).wait_send()
-            pl.when(sends_far(n))(lambda: far_copy(n).wait_send())
+    @pl.loop(0, pieces)
+    def _(n):
+        for d in range(3):
+            i = (2 - d) * pieces + n
+            for side in range(2):
+                pl.when(sends_core(d, side))(lambda: core_copy(i, side).wait_send())
+            pl.when(sends_pair(d, n))(lambda: pair_copy(i).wait_send())
+            if d > 0:
+                when(sends_layer(d, n))(lambda: layer_copy(i).wait_send())
+        rep_copy(n).wait_send()
+        pl.when(sends_far(n))(lambda: far_copy(n).wait_send())
 
     for d in range(3):
         for side in range(2):
             pl.when(sends_core(d, side))(lambda: core_part_copy(d, side).wait_send())
         pl.when(sends_pair(d))(lambda: pair_part_copy(d).wait_send())
         if d > 0:
-            pl.when(sends_layer(d))(lambda: layer_part_copy(d).wait_send())
+            when(sends_layer(d))(lambda: layer_part_copy(d).wait_send())
     rep_part_copy().wait_send()
     for away in range(1, layers):
         spread(away).wait_send()
@@ -935,11 +937,10 @@
         return remote(slots.at[1, whose, h, span(p)], slots.at[2, whose, h, span(p)],
                       far_sems, (h, p), onward)
 
+    chip_far, layer_far = at.chip_meets(at.pair, lane, 2), at.layer_meets(lane, 2)
+
     def sends_layer(p):
-        return jnp.logical_or(
-            at.chip_meets(at.pair, lane, 2),
-            jnp.logical_and(p < by_pair, at.layer_meets(lane, 2)),
-        )
+        return jnp.logical_or(chip_far, jnp.logical_and(p < by_pair, layer_far))
 
     def sends_far(p):
         return jnp.logical_and(p >= by_pair, gets["pair"](2))
@@ -948,15 +949,18 @@
         holds = kind["pair"](d)
         return jnp.logical_and(p < by_pair, holds) if d == 2 else holds
 
+    def fixed(test):
+        return [test(d) for d in range(3)].__getitem__
+
     sends = {
-        "pair": lambda d: at.chip_meets(1 - at.pair, lane, d),
-        "core": lambda d: at.meets(at.lane_beside, lane, d),
-        "relay": lambda d: at.meets(at.lane_beside, at.lane_across, d),
+        "pair": fixed(lambda d: at.chip_meets(1 - at.pair, lane, d)),
+        "core": fixed(lambda d: at.meets(at.lane_beside, lane, d)),
+        "relay": fixed(lambda d: at.meets(at.lane_beside, at.lane_across, d)),
     }
     gets = {
-        "pair": lambda d: at.chip_meets(at.pair, at.lane_across, d),
-        "core": lambda d: at.meets(lane, at.lane_beside, d),
-        "relay": lambda d: at.meets(lane, diagonal, d),
+        "pair": fixed(lambda d: at.chip_meets(at.pair, at.lane_across, d)),
+        "core": fixed(lambda d: at.meets(lane, at.lane_beside, d)),
+        "relay": fixed(lambda d: at.meets(lane, diagonal, d)),
     }
 
     def give(h, d, p, kinds):
@@ -1057,10 +1061,10 @@
     arrive(0)
     whole(0, 1)
     relay(1, 1)
+    whole(1, 0)
     relay(0, 2)
     last(0)
     arrive(1)
-    whole(1, 0)
     whole(1, 1)
     relay(1, 2)
     last(1)

time: 99.3 us -> 97.8 us (0.985)
  Pallas kernels: 91.3 us -> 90.2 us
    pallas_call x1, Pallas kernels: 77.2 us -> 76 us  [layered(): pl.pallas_call(functools.partial(layered_kernel, cycle, pieces, back_piec...]
where the time goes in v2:
time: 97.8 us; the launch traced here: 97.5 us
  Pallas kernels  90.2 us (92%)
  starting transfers between devices  6.55 us (7%)
    pallas_call x1, Pallas kernels, layered(): pl.pallas_call(functools.partial(layered_kernel, cycle, pieces, back_piec...  76 us
    pallas_call x1, Pallas kernels, build_dense(): pl.pallas_call(build_kernel, grid_spec=pltpu.PrefetchScalarGridSpec(num_s...  13 us
    ppermute x2, starting transfers between devices, ahead_of_build(): lax.ppermute(features, ('blk', 'rep'), pairs)  6.55 us
  transfers between devices with their start and end apart: 2, of which 0 were waited for; matrix products, arithmetic and copies ran while one was open for 0% of the time, Pallas kernels for 13%

profile of v2, /device:TPU:0, one launch (start us, length us, event | category | flops | bytes accessed | tf_op | source)
XLA Modules:
  0.0 97.5 jit_solution(15541155352617812319)
XLA Ops:
  0.6 0.0 copy-start
  0.6 0.0 copy-start.1
  0.7 0.0 copy-start.4
  0.7 0.0 copy-start.3
  0.7 0.0 copy-start.2
  0.7 3.1 %collective-permute-start = (bf16[1024,256]{1,0:T(8,128)(2,1)}, bf16[1024,256]{1,0:T(8,128)(2,1)S(1)}, u32[]{:S(2)}, u32[]{:S(2)}) collective-permute-start(bf16[1024,256]{1,0:T(8,128)(2,1)} %features.1), channel_id=1, source_target_pairs={{0,8},{1,25},{2,10},{3,27},{4,12},{5,29},{6,14},{7,31},{8,16},{9,1... | collective-permute-start | bytes 1572872 | tf_op jit(solution)/shard_map/ppermute | solution.py:1154
  3.8 3.4 %collective-permute-start.1 = (bf16[1024,256]{1,0:T(8,128)(2,1)}, bf16[1024,256]{1,0:T(8,128)(2,1)S(1)}, u32[]{:S(2)}, u32[]{:S(2)}) collective-permute-start(bf16[1024,256]{1,0:T(8,128)(2,1)} %features.1), channel_id=1, source_target_pairs={{0,4},{2,6},{5,1},{7,3},{8,12},{10,14},{13,9},{15,11},{16,20},{18,... | collective-permute-start | bytes 1572872 | tf_op jit(solution)/shard_map/ppermute | solution.py:1154
  7.2 13.0 %build.1.dense = bf16[8,1024,1024]{2,1,0:T(8,128)(2,1)} custom-call(s32[8,64]{1,0:T(8,128)} %bitcast.7, s32[8,64]{1,0:T(8,128)} %bitcast.8, s32[8,64]{1,0:T(8,128)} %bitcast.9, s32[8]{0:T(128)} %bitcast.10, bf16[128,128,128]{2,1,0:T(8,128)(2,1)} %table.1), custom_call_target="tpu_custom_call" | custom-call | bytes 20971520 | tf_op jit(solution)/shard_map/build/pallas_call | solution.py:31
  20.2 0.0 collective-permute-done.behind
  20.3 0.0 collective-permute-done.1.across
  20.3 0.0 copy-done
  20.3 0.0 copy-done.1
  20.3 0.0 copy-done.4
  20.3 0.0 copy-done.3
  20.3 0.0 copy-done.2
  20.3 76.0 %layered.1 = (bf16[1024,256]{1,0:T(8,128)(2,1)S(1)}, bf16[1024,256]{1,0:T(8,128)(2,1)S(1)}, f32[256,256]{1,0:T(8,128)S(1)}, f32[256,256]{1,0:T(8,128)S(1)}, f32[1,256]{1,0:T(1,128)S(1)}) custom-call(bf16[1024,256]{1,0:T(8,128)(2,1)S(1)} %copy-done, bf16[1024,256]{1,0:T(8,128)(2,1)S(1)} %collective-permute-done.behind, ...), custom_call_target="tpu_custom_call" | custom-call | tf_op jit(solution)/shard_map/layered/pallas_call | solution.py:1171
  96.3 1.2 %close.1 = (bf16[1024,256]{1,0:T(8,128)(2,1)}, bf16[1024,256]{1,0:T(8,128)(2,1)}, f32[256,256]{1,0:T(8,128)}, f32[256,256]{1,0:T(8,128)}, f32[1,256]{1,0:T(1,128)}) custom-call(bf16[1024,256]{1,0:T(8,128)(2,1)S(1)} %get-tuple-element.15.refs_0_, bf16[1024,256]{1,0:T(8,128)(2,1)S(1)} %get-tuple-element.16.refs_1_, f32[256,256]{1,0:T(8,128)S(1)} %get-tuple-element.17.refs_2_, ...), custom_call_target="tpu_custom_call" | custom-call | tf_op jit(solution)/shard_map/close/pallas_call | solution.py:1211
Async XLA Ops:
  0.6 19.6 %copy-start = (bf16[1024,256]{1,0:T(8,128)(2,1)S(1)}, bf16[1024,256]{1,0:T(8,128)(2,1)}, u32[]{:S(2)}) copy-start(bf16[1024,256]{1,0:T(8,128)(2,1)} %features.1) | copy-start | bytes 1572868
  0.6 19.6 %copy-start.1 = (bf16[1024,256]{1,0:T(8,128)(2,1)S(1)}, bf16[1024,256]{1,0:T(8,128)(2,1)}, u32[]{:S(2)}) copy-start(bf16[1024,256]{1,0:T(8,128)(2,1)} %cotangent.1) | copy-start | bytes 1572868
  0.7 19.6 %copy-start.4 = (f32[256]{0:T(256)S(1)}, f32[256]{0:T(256)}, u32[]{:S(2)}) copy-start(f32[256]{0:T(256)} %param.13) | copy-start | bytes 3076
  0.7 19.6 %copy-start.3 = (bf16[256,256]{1,0:T(8,128)(2,1)S(1)}, bf16[256,256]{1,0:T(8,128)(2,1)}, u32[]{:S(2)}) copy-start(bf16[256,256]{1,0:T(8,128)(2,1)} %weight_neighbor.1) | copy-start | bytes 393220
  0.7 19.6 %copy-start.2 = (bf16[256,256]{1,0:T(8,128)(2,1)S(1)}, bf16[256,256]{1,0:T(8,128)(2,1)}, u32[]{:S(2)}) copy-start(bf16[256,256]{1,0:T(8,128)(2,1)} %weight_self.1) | copy-start | bytes 393220
  0.7 19.6 %collective-permute-start = (bf16[1024,256]{1,0:T(8,128)(2,1)}, bf16[1024,256]{1,0:T(8,128)(2,1)S(1)}, u32[]{:S(2)}, u32[]{:S(2)}) collective-permute-start(bf16[1024,256]{1,0:T(8,128)(2,1)} %features.1), channel_id=1, source_target_pairs={{0,8},{1,25},{2,10},{3,27},{4,12},{5,29},{6,14},{7,31},{8,16},{9,1... | collective-permute-start | bytes 1572872 | tf_op jit(solution)/shard_map/ppermute | solution.py:1154
  3.8 16.5 %collective-permute-start.1 = (bf16[1024,256]{1,0:T(8,128)(2,1)}, bf16[1024,256]{1,0:T(8,128)(2,1)S(1)}, u32[]{:S(2)}, u32[]{:S(2)}) collective-permute-start(bf16[1024,256]{1,0:T(8,128)(2,1)} %features.1), channel_id=1, source_target_pairs={{0,4},{2,6},{5,1},{7,3},{8,12},{10,14},{13,9},{15,11},{16,20},{18,... | collective-permute-start | bytes 1572872 | tf_op jit(solution)/shard_map/ppermute | solution.py:1154
